TPU v7x, 32 devices: a whole 2x2x4 slice. The times are simulated.
32 devices in a mesh: expert: 4 (over z), ctx: 4 (over y, x), dp: 2 (over core).
Axes of the slice: x: 2, y: 2, z: 4, core: 2. Of those that a mesh axis runs over, the one named last changes fastest.
Arguments:
- tokens: bfloat16 [8, 1024, 1024], P(('expert', 'dp'), 'ctx'), may hold values from -6 to 6
- out_grad: bfloat16 [8, 1024, 1024], P(('expert', 'dp'), 'ctx'), may hold values from -6 to 6
- token_ids: int32 [8, 1024], P(('expert', 'dp'), 'ctx'), may hold values from 0 to 32767, as said below
- hash_table: int32 [32768], replicated, may hold values from 0 to 3, as said below
- doc_lengths: int32 [8, 8], P(('expert', 'dp')), may hold values from 1 to 896, 1024 in all within a row
- w_qkv: bfloat16 [1024, 3072], replicated, may hold values from -0.1875 to 0.1875
- w_out: bfloat16 [1024, 1024], replicated, may hold values from -3 to 3
- gain_attn: float32 [1024], replicated, may hold values from 0.5 to 1.5
- gain_ffn: float32 [1024], replicated, may hold values from 0.5 to 1.5
- expert_in: bfloat16 [4, 1024, 4096], P('expert', None, ('ctx', 'dp')), may hold values from -0.1875 to 0.1875
- expert_out: bfloat16 [4, 4096, 1024], P('expert', ('ctx', 'dp')), may hold values from -0.09375 to 0.09375
Outputs:
- block_out: bfloat16 [8, 1024, 1024], P(('expert', 'dp'), 'ctx')
- grad_tokens: float32 [8, 1024, 1024], P(('expert', 'dp'), 'ctx')
- grad_w_qkv: float32 [1024, 3072], replicated
- grad_w_out: float32 [1024, 1024], replicated
- grad_gain_attn: float32 [1024], replicated
- grad_gain_ffn: float32 [1024], replicated
- grad_expert_in: float32 [4, 1024, 4096], P('expert', None, ('ctx', 'dp'))
- grad_expert_out: float32 [4, 4096, 1024], P('expert', ('ctx', 'dp'))
Inputs may be any that keep to these rules, and one draw needn't show every extreme that they name: hash_table names every expert for exactly 8192 ids. `token_ids`: of the 256 tokens of one device, at most 80 map to one expert through hash_table, and in every device exactly 80 map to some expert.
All inputs are finite; a program needn't handle non-finite values.
Results may differ from a plain program's by a relative error of at most 0.012.
Values may be sent and summed in bfloat16 or wider, within the bound.
No kernel may reach another device: no remote copies, remote signals or barrier semaphores. Data moves between devices by JAX's collectives and lax.ppermute only.
A program may use at most 192 MiB of HBM per device.

v0:
```python
import functools
import jax
import jax.numpy as jnp
from jax import lax
from jax.experimental import pallas as pl
from jax.experimental.pallas import tpu as pltpu
from jax.sharding import PartitionSpec as P

HEADS = 16
HEAD = 64
PAIR = 2 * HEAD

eps = 1e-06
score_scale = 0.125
F32 = jnp.float32
BF16 = jnp.bfloat16
VMEM = pl.BlockSpec(memory_space=pltpu.VMEM)
SMEM = pl.BlockSpec(memory_space=pltpu.SMEM)
shaped = jax.ShapeDtypeStruct


def swap(value, axis, bits):
    size = lax.axis_size(axis)
    return lax.ppermute(value, axis, [(i, i ^ bits) for i in range(size)])


def exchange(value, axis):
    return lax.all_to_all(value, axis, split_axis=0, concat_axis=0, tiled=True)


def spread_to(value, axis):
    return exchange(jnp.broadcast_to(value[None], (lax.axis_size(axis),) + value.shape), axis)


def after(value, *others):
    return lax.optimization_barrier((value,) + others)[0]


def matmul(a, b):
    return jnp.dot(a, b, preferred_element_type=F32)


def matmul_nt(a, b):
    return lax.dot_general(a, b, (((1,), (1,)), ((), ())), preferred_element_type=F32)


def matmul_tn(a, b):
    return lax.dot_general(a, b, (((0,), (0,)), ((), ())), preferred_element_type=F32)


def params(mib):
    return pltpu.CompilerParams(vmem_limit_bytes=mib << 20)


def cost(flops, moved, transcendentals=0):
    return pl.CostEstimate(
        flops=int(flops / 4), bytes_accessed=int(moved / 4), transcendentals=int(transcendentals / 4)
    )


def distances(bits):
    found = [0]
    for bit in reversed(bits):
        found = found + [value ^ bit for value in found]
    return found


def gelu_parts(pre):
    c = 0.7978845608028654
    square = pre * pre
    t = jnp.tanh(c * (pre + 0.044715 * pre * square))
    half = 0.5 * (1.0 + t)
    slope = half + 0.5 * pre * (1.0 - t * t) * (c * (1.0 + 3.0 * 0.044715 * square))
    return pre * half, slope


def forward_kernel(ids_ref, ends_ref, gain_ref, *refs, n, rows):
    blocks = refs[:n]
    weights = refs[n : n + 3]
    normed_ref, inv_ref, q_ref, k_ref, v_ref, mixed_ref, att_ref, tot_ref = refs[n + 3 :]
    rank = ids_ref[0]
    pairs = mixed_ref.shape[1] // PAIR
    for r in range(n):
        x = blocks[r][...].astype(F32)
        inverse = lax.rsqrt(jnp.mean(x * x, axis=-1, keepdims=True) + eps)
        if r == 0:
            inv_ref[...] = inverse
        here = pl.ds(pl.multiple_of((rank ^ r) * rows, rows), rows)
        normed = (x * inverse * gain_ref[...]).astype(BF16)
        normed_ref[here, :] = normed
        q_ref[here, :] = (matmul(normed, weights[0][...]) * score_scale).astype(BF16)
        k_ref[here, :] = matmul(normed, weights[1][...]).astype(BF16)
        v_ref[here, :] = matmul(normed, weights[2][...]).astype(BF16)
    low = lax.broadcasted_iota(jnp.int32, (rows, PAIR), 1) < HEAD
    q_iota = lax.broadcasted_iota(jnp.int32, (rows, rows), 0)
    k_iota = lax.broadcasted_iota(jnp.int32, (rows, rows), 1)
    one = jnp.ones((), BF16)
    zero = jnp.zeros((), BF16)

    @pl.loop(0, pairs)
    def _(p):
        out = pl.ds(pl.multiple_of(p * PAIR, PAIR), PAIR)
        for i in range(n):
            q_at = slice(i * rows, (i + 1) * rows)
            q2 = q_ref[q_at, out]
            qs = (jnp.where(low, q2, zero), jnp.where(low, zero, q2))
            sums = [None, None]
            for j in range(i + 1):
                k_at = slice(j * rows, (j + 1) * rows)
                k2 = k_ref[k_at, out]
                v2 = v_ref[k_at, out]
                vs = (jnp.where(low, v2, one), jnp.where(low, one, v2))
                seen = q_iota + i * rows < ends_ref[:, j * rows : (j + 1) * rows]
                if i == j:
                    seen = seen & (k_iota <= q_iota)
                for h in range(2):
                    w = jnp.where(seen, jnp.exp(matmul_nt(qs[h], k2)), 0.0).astype(BF16)
                    part = matmul(w, vs[h])
                    sums[h] = part if sums[h] is None else sums[h] + part
            total = jnp.where(low, pltpu.roll(sums[0], HEAD, 1), pltpu.roll(sums[1], HEAD, 1))
            att = jnp.where(low, sums[0], sums[1]) / total
            att_ref[q_at, out] = att
            mixed_ref[q_at, out] = att.astype(BF16)
            tot_ref[q_at, out] = total


def attend_forward(ids, ends, gain, blocks, w_qkv, n):
    rows, width = blocks[0].shape
    group = width // n
    length = n * rows
    count = n * (n + 1) // 2 * (group // HEAD)

    def whole(*shape):
        return pl.BlockSpec(shape, lambda s, ids_ref: (0, 0))

    def columns(part):
        return pl.BlockSpec((width, group), lambda s, ids_ref: (0, part * n + ids_ref[0]))

    own = (length, group)
    return pl.pallas_call(
        functools.partial(forward_kernel, n=n, rows=rows),
        out_shape=(
            shaped((length, width), BF16),
            shaped((rows, 1), F32),
            shaped(own, BF16),
            shaped(own, BF16),
            shaped(own, BF16),
            shaped(own, BF16),
            shaped(own, F32),
            shaped(own, F32),
        ),
        grid_spec=pltpu.PrefetchScalarGridSpec(
            num_scalar_prefetch=1,
            grid=(1,),
            in_specs=[whole(1, length), whole(1, width)]
            + [whole(rows, width)] * n
            + [columns(0), columns(1), columns(2)],
            out_specs=[whole(length, width), whole(rows, 1)] + [whole(*own)] * 6,
        ),
        compiler_params=params(48),
        cost_estimate=cost(
            count * rows * rows * PAIR * 4 + 6 * length * width * group,
            length * width * 4 + length * group * 16 + 6 * width * group,
            count * rows * rows,
        ),
    )(ids, ends, gain, *blocks, w_qkv, w_qkv, w_qkv)


def middle_kernel(ids_ref, *refs, n):
    parts = refs[:n]
    w_ref, x_ref, gain_ref, picks_ref, hidden_ref, inv_ref, sent_ref = refs[n:]
    group = parts[0].shape[1]
    hidden = x_ref[...].astype(F32)
    for r in range(n):
        at = pl.ds(pl.multiple_of((ids_ref[0] ^ r) * group, group), group)
        hidden = hidden + matmul(parts[r][...], w_ref[at, :])
    hidden_ref[...] = hidden
    inverse = lax.rsqrt(jnp.mean(hidden * hidden, axis=-1, keepdims=True) + eps)
    inv_ref[...] = inverse
    low = (hidden * inverse * gain_ref[...]).astype(BF16)
    sent_ref[...] = matmul(picks_ref[...], low).astype(BF16)


def middle(ids, parts, w_out, x, gain, picks):
    rows, width = x.shape
    slots = picks.shape[0]
    return pl.pallas_call(
        functools.partial(middle_kernel, n=len(parts)),
        out_shape=(
            shaped((rows, width), F32),
            shaped((rows, 1), F32),
            shaped((slots, width), BF16),
        ),
        in_specs=[SMEM] + [VMEM] * (len(parts) + 4),
        out_specs=(VMEM, VMEM, VMEM),
        compiler_params=params(24),
        cost_estimate=cost(2 * rows * width * (width + slots), 6 * width * width),
    )(ids, *parts, w_out, x, gain, picks)


def place_columns(out_ref, where, rest_ref, units):
    width = out_ref.shape[1]
    for b in range(width // units):
        at = rest_ref.shape[0] - width + b * units
        out_ref[where, b * units : (b + 1) * units] = rest_ref[at : at + units]


def expert_kernel(*refs, m):
    row_ref, up_ref, w_in, w_out = refs[:4]
    firsts, rests = refs[4 : 4 + m], refs[4 + m : 4 + 2 * m]
    own_ref, other_ref, act_out, pre_out, in_ref, out_ref, act_ref, pre_ref, sems = refs[4 + 2 * m :]
    width, units = w_in.shape
    in_ref[:, :units] = w_in[...]
    out_ref[:units, :] = w_out[...]
    for i in range(m):
        cols = slice((i + 1) * units, (i + 2) * units)
        top = firsts[i].shape[0]
        in_ref[:top, cols] = firsts[i][...]
        in_ref[top:, cols] = rests[i][: width - top]
        place_columns(out_ref, cols, rests[i], units)
    half = own_ref.shape[0]
    size = half

    @pl.loop(0, 2 * half // size)
    def _(i):
        here = pl.ds(pl.multiple_of(i * size, size), size)
        value, slope = gelu_parts(matmul(row_ref[here, :], in_ref[...]))
        act_ref[here, :] = value.astype(BF16)
        grad_pre = (slope * matmul_nt(up_ref[here, :], out_ref[...])).astype(BF16)
        pre_ref[here, :] = grad_pre
        part = matmul_nt(grad_pre, in_ref[...]).astype(BF16)

        @pl.when(i * size < half)
        def _():
            own_ref[here, :] = part

        @pl.when(i * size >= half)
        def _():
            other_ref[pl.ds(pl.multiple_of(i * size - half, size), size), :] = part

    keep_act = pltpu.make_async_copy(act_ref, act_out, sems.at[0])
    keep_act.start()
    keep_pre = pltpu.make_async_copy(pre_ref, pre_out, sems.at[1])
    keep_pre.start()
    keep_act.wait()
    keep_pre.wait()


def expert_rows(row_chunk, up_chunk, w_in, w_out, firsts, rests):
    count, width = row_chunk.shape
    m = len(firsts)
    hidden = (m + 1) * w_in.shape[1]
    anywhere = pl.BlockSpec(memory_space=pl.ANY)
    return pl.pallas_call(
        functools.partial(expert_kernel, m=m),
        out_shape=[shaped((count // 2, width), BF16)] * 2 + [shaped((count, hidden), BF16)] * 2,
        in_specs=[VMEM] * (4 + 2 * m),
        out_specs=[VMEM] * 2 + [anywhere] * 2,
        scratch_shapes=[
            pltpu.VMEM((width, hidden), BF16),
            pltpu.VMEM((hidden, width), BF16),
            pltpu.VMEM((count, hidden), BF16),
            pltpu.VMEM((count, hidden), BF16),
            pltpu.SemaphoreType.DMA((2,)),
        ],
        compiler_params=params(40),
        cost_estimate=cost(6 * count * width * hidden, 4 * width * hidden + 8 * count * width),
    )(row_chunk, up_chunk, w_in, w_out, *firsts, *rests)


def turn_kernel(ids_ref, *refs, n, owners):
    backs, mixed = refs[:owners], refs[owners : owners + n]
    places_ref, hidden_ref, up_ref, inv_ref, gain_ref, w_ref = refs[owners + n : owners + n + 6]
    grad_ref, part_ref, mine_ref, theirs_ref, branch_ref, full_ref, mixed_ref = refs[owners + n + 6 :]
    group = part_ref.shape[2]
    width = hidden_ref.shape[1]
    grad_rows = None
    for k in range(owners):
        term = matmul(places_ref[k], backs[k][...])
        grad_rows = term if grad_rows is None else grad_rows + term
    hidden = hidden_ref[...]
    inverse = inv_ref[...]
    scaled = grad_rows * gain_ref[...]
    inner = jnp.mean(scaled * hidden, axis=-1, keepdims=True)
    grad = up_ref[...].astype(F32) + inverse * scaled - hidden * (inverse**3 * inner)
    grad_ref[...] = grad
    branch_ref[...] = grad.astype(BF16)
    for r in range(n):
        at = pl.ds(pl.multiple_of((ids_ref[0] ^ r) * group, group), group)
        part_ref[r] = matmul_nt(branch_ref[...], w_ref[at, :]).astype(BF16)
    sums = jnp.sum(grad_rows * hidden * inverse, axis=0, keepdims=True)
    blocks = width // (2 * PAIR)
    piece = group // owners
    for r in range(n):
        mixed_ref[r] = mixed[r][...]

    @pl.loop(0, n)
    def _(r):
        full_ref[...] = matmul_tn(mixed_ref[r], branch_ref[...])
        for s, out_ref in ((0, mine_ref), (1, theirs_ref)):
            for k in range(owners):
                row_at = pl.ds(pl.multiple_of((ids_ref[1] ^ k) * piece, piece), piece)
                for b in range(blocks):
                    col = pl.multiple_of(((ids_ref[2] ^ s) * blocks + b) * PAIR, PAIR)
                    at = pl.multiple_of(((r * owners + k) * blocks + b) * piece, piece)
                    out_ref[pl.ds(at, piece), :] = full_ref[row_at, pl.ds(col, PAIR)].astype(
                        out_ref.dtype
                    )
    size = mine_ref.shape[0]
    cols = width // PAIR
    lines = [sums[:, i * PAIR : (i + 1) * PAIR] for i in range(cols)]
    lines = jnp.concatenate(lines + [jnp.zeros((-cols % 16, PAIR), F32)], axis=0)
    theirs_ref[size : size + lines.shape[0], :] = lines.astype(BF16)


def turn(ids, backs, mixed, places, hidden, up, inverse, gain, w_out):
    rows, width = hidden.shape
    n = len(mixed)
    size = width * width // (2 * PAIR)
    extra = -(-width // PAIR // 16) * 16
    return pl.pallas_call(
        functools.partial(turn_kernel, n=n, owners=len(backs)),
        out_shape=(
            shaped((rows, width), F32),
            shaped((n, rows, width // n), BF16),
            shaped((size, PAIR), F32),
            shaped((size + extra, PAIR), BF16),
        ),
        in_specs=[SMEM] + [VMEM] * (len(backs) + n + 6),
        out_specs=(VMEM,) * 4,
        scratch_shapes=[pltpu.VMEM((rows, width), BF16), pltpu.VMEM((width // n, width), F32), pltpu.VMEM((n, rows, width // n), BF16)],
        compiler_params=params(32),
        cost_estimate=cost(4 * rows * width * (width + rows), 10 * width * width),
    )(ids, *backs, *mixed, places, hidden, up, inverse, gain, w_out)


def weight_grad_kernel(*refs, chunks, sizes):
    a_refs = refs[:chunks]
    b_refs = refs[chunks : 2 * chunks]
    outs = refs[2 * chunks :]
    total = None
    for a_ref, b_ref in zip(a_refs, b_refs):
        term = matmul_tn(a_ref[...], b_ref[...])
        total = term if total is None else total + term
    at = 0
    for out_ref, size in zip(outs, sizes):
        out_ref[...] = total[:, at : at + size].astype(out_ref.dtype)
        at += size


def weight_grads(row_chunks, per_chunk, sizes):
    width = row_chunks[0].shape[1]
    tile = 256
    total = sum(chunk.shape[0] for chunk in row_chunks)
    return pl.pallas_call(
        functools.partial(weight_grad_kernel, chunks=len(row_chunks), sizes=sizes),
        out_shape=[shaped((width, size), BF16 if i else F32) for i, size in enumerate(sizes)],
        grid=(width // tile,),
        in_specs=[pl.BlockSpec((chunk.shape[0], tile), lambda i: (0, i)) for chunk in row_chunks]
        + [pl.BlockSpec(value.shape, lambda i: (0, 0)) for value in per_chunk],
        out_specs=[pl.BlockSpec((tile, size), lambda i: (i, 0)) for size in sizes],
        compiler_params=params(40),
        cost_estimate=cost(2 * width * sum(sizes) * total, 8 * width * sum(sizes)),
    )(*row_chunks, *per_chunk)


def weight_out_kernel(*refs, chunks, sizes, tile):
    acts = refs[:chunks]
    ups = refs[chunks : 2 * chunks]
    outs = refs[2 * chunks :]
    total = None
    for act, up in zip(acts, ups):
        term = matmul_tn(act[...], up[...])
        total = term if total is None else total + term
    first = 0
    for out_ref, size in zip(outs, sizes):
        steps = size // tile

        @pl.when((pl.program_id(0) >= first) & (pl.program_id(0) < first + steps))
        def _():
            out_ref[...] = total.astype(out_ref.dtype)

        first += steps


def weight_grads_out(acts, up_chunks, sizes):
    width = up_chunks[0].shape[1]
    tile = min(256, min(sizes))
    total = sum(chunk.shape[0] for chunk in up_chunks)
    specs = []
    first = 0
    for size in sizes:
        steps = size // tile
        specs.append(
            pl.BlockSpec(
                (tile, width), lambda i, first=first, steps=steps: (jnp.clip(i - first, 0, steps - 1), 0)
            )
        )
        first += steps
    return pl.pallas_call(
        functools.partial(weight_out_kernel, chunks=len(acts), sizes=sizes, tile=tile),
        out_shape=[shaped((size, width), BF16 if i else F32) for i, size in enumerate(sizes)],
        grid=(first,),
        in_specs=[pl.BlockSpec((act.shape[0], tile), lambda i: (0, i)) for act in acts]
        + [pl.BlockSpec(chunk.shape, lambda i: (0, 0)) for chunk in up_chunks],
        out_specs=specs,
        compiler_params=params(40),
        cost_estimate=cost(2 * width * sum(sizes) * total, 8 * width * sum(sizes)),
    )(*acts, *up_chunks)


def produce_kernel(*refs, chunks, m, sizes):
    acts = refs[:chunks]
    w_out = refs[chunks]
    rests = refs[chunks + 1 : chunks + 1 + m]
    own_ref, other_ref, out_ref = refs[chunks + 1 + m :]
    units, width = w_out.shape
    out_ref[:units, :] = w_out[...]
    for i in range(m):
        cols = slice((i + 1) * units, (i + 2) * units)
        place_columns(out_ref, cols, rests[i], units)
    at = 0
    for c in range(chunks):
        size = sizes[c]

        @pl.loop(0, 2)
        def _(h):
            here = pl.ds(pl.multiple_of(h * 2 * size, 2 * size), 2 * size)
            total = matmul(acts[c][here, :], out_ref[...]).astype(BF16)

            @pl.when(h == 0)
            def _():
                for b in range(2):
                    own_ref[b, at : at + size, :] = total[b * size : (b + 1) * size]

            @pl.when(h == 1)
            def _():
                for b in range(2):
                    other_ref[b, at : at + size, :] = total[b * size : (b + 1) * size]

        at += size


def produce(acts, w_out, rests, sizes):
    width = w_out.shape[1]
    hidden = acts[0].shape[1]
    shape = (2, sum(sizes), width)
    return pl.pallas_call(
        functools.partial(produce_kernel, chunks=len(acts), m=len(rests), sizes=sizes),
        out_shape=(shaped(shape, BF16), shaped(shape, BF16)),
        in_specs=[VMEM] * (len(acts) + 1 + len(rests)),
        out_specs=(VMEM, VMEM),
        scratch_shapes=[pltpu.VMEM((hidden, width), BF16)],
        compiler_params=params(40),
        cost_estimate=cost(
            8 * sum(sizes) * width * hidden, 2 * hidden * width + 16 * sum(sizes) * width
        ),
    )(*acts, w_out, *rests)


def backward_kernel(
    ids_ref,
    starts_ref,
    normed_ref,
    q_ref,
    k_ref,
    v_ref,
    att_ref,
    tot_ref,
    g_ref,
    *refs,
    n,
    rows,
    owners,
):
    out_ref, mine_ref, theirs_ref, dq_ref, do_ref, sh_ref, full_ref = refs
    rank = ids_ref[0]
    pairs = q_ref.shape[1] // PAIR
    low = lax.broadcasted_iota(jnp.int32, (rows, PAIR), 1) < HEAD
    k_iota = lax.broadcasted_iota(jnp.int32, (rows, rows), 0)
    q_iota = lax.broadcasted_iota(jnp.int32, (rows, rows), 1)
    zero = jnp.zeros((), BF16)

    def both(value):
        return jnp.where(low, value, zero), jnp.where(low, zero, value)

    @pl.loop(0, pairs)
    def _(p):
        cols = pl.ds(pl.multiple_of(p * PAIR, PAIR), PAIR)
        for i in range(n):
            here = slice(i * rows, (i + 1) * rows)
            at = pl.ds(pl.multiple_of((rank ^ i) * rows, rows), rows)
            scaled = g_ref[at, cols].astype(F32) / tot_ref[here, cols]
            do_ref[here, :] = scaled.astype(BF16)
            turned = (scaled * att_ref[here, cols]).T
            sh_ref[0:1, here] = jnp.sum(turned[:HEAD], axis=0, keepdims=True)
            sh_ref[1:2, here] = jnp.sum(turned[HEAD:], axis=0, keepdims=True)
        for j in range(n):
            k_at = slice(j * rows, (j + 1) * rows)
            k2 = k_ref[k_at, cols]
            v2 = v_ref[k_at, cols]
            ks = both(k2)
            dk = None
            dv = None
            for i in range(j, n):
                here = slice(i * rows, (i + 1) * rows)
                qs = both(q_ref[here, cols])
                dos = both(do_ref[here, :])
                seen = k_iota + j * rows >= starts_ref[:, here]
                if i == j:
                    seen = seen & (k_iota <= q_iota)
                dq = None
                for h in range(2):
                    weights = jnp.where(seen, jnp.exp(matmul_nt(k2, qs[h])), 0.0)
                    slope = matmul_nt(v2, dos[h]) - sh_ref[h : h + 1, here]
                    ds = (weights * slope).astype(BF16)
                    dv_part = matmul(weights.astype(BF16), dos[h])
                    dk_part = matmul(ds, qs[h])
                    dq_part = matmul_tn(ds, ks[h])
                    dv = dv_part if dv is None else dv + dv_part
                    dk = dk_part if dk is None else dk + dk_part
                    dq = dq_part if dq is None else dq + dq_part
                if j == 0:
                    dq_ref[here, :] = dq
                else:
                    dq_ref[here, :] += dq
            out_ref[j, 1, :, cols] = dk.astype(BF16)
            out_ref[j, 2, :, cols] = dv.astype(BF16)
            out_ref[j, 0, :, cols] = (dq_ref[k_at, :] * score_scale).astype(BF16)

    @pl.loop(0, 3)
    def _(part):
        total = None
        for j in range(n):
            term = matmul_tn(normed_ref[j * rows : (j + 1) * rows, :], out_ref[j, part])
            total = term if total is None else total + term
        full_ref[part] = total

    piece = full_ref.shape[1] // (2 * owners)
    for s, to_ref in ((0, mine_ref), (1, theirs_ref)):
        for k in range(owners):
            row = ((ids_ref[2] ^ s) * owners + (ids_ref[1] ^ k)) * piece
            row_at = pl.ds(pl.multiple_of(row, piece), piece)
            for part in range(3):
                for p in range(pairs):
                    at = (part * pairs + p) * piece
                    to_ref[k, at : at + piece, :] = full_ref[
                        part, row_at, p * PAIR : (p + 1) * PAIR
                    ].astype(to_ref.dtype)


def attend_backward(ids, starts, normed, q, k, v, att, tot, g, n, owners):
    length, width = normed.shape
    group = q.shape[1]
    rows = length // n
    count = n * (n + 1) // 2 * (group // HEAD)
    size = (owners, width // (2 * owners) * 3 * group // PAIR, PAIR)
    return pl.pallas_call(
        functools.partial(backward_kernel, n=n, rows=rows, owners=owners),
        out_shape=(
            shaped((n, 3, rows, group), BF16),
            shaped(size, F32),
            shaped(size, BF16),
        ),
        in_specs=[SMEM] + [VMEM] * 8,
        out_specs=(VMEM,) * 3,
        scratch_shapes=[
            pltpu.VMEM((length, PAIR), F32),
            pltpu.VMEM((length, PAIR), BF16),
            pltpu.VMEM((8, length), F32),
            pltpu.VMEM((3, width, group), F32),
        ],
        compiler_params=params(48),
        cost_estimate=cost(
            count * rows * rows * PAIR * 10 + 6 * length * width * group,
            length * group * 24 + 2 * length * width + 9 * width * group,
            count * rows * rows,
        ),
    )(ids, starts, normed, q, k, v, att, tot, g)


def join_kernel(*refs, owners):
    mine_ref, got_ref, out_ref, near_ref = refs[:4]
    count = len(refs) - 4 - owners - 1
    others = refs[4 : 4 + count]
    own_ref, gain_ref = refs[4 + count : 6 + count]
    sent = refs[6 + count :]
    rows = mine_ref.shape[1]
    size = out_ref.shape[0]
    tall = size // owners
    out = out_ref[...]
    gains = [near_ref[...].astype(F32)]
    for other in others:
        out = out + other[:size, :].astype(F32)
        gains.append(other[size:, :].astype(F32))
    while len(gains) > 1:
        gains = [gains[i] + gains[i + 1] for i in range(0, len(gains), 2)]
    gain = gains[0].astype(BF16)
    gain_ref[...] = gain
    for k in range(owners):
        total = mine_ref[k] + got_ref[k].astype(F32)
        part = out[k * tall : (k + 1) * tall]
        if k == 0:
            own_ref[:rows, :] = total
            own_ref[rows:, :] = part
        else:
            sent[k - 1][:rows, :] = total.astype(BF16)
            sent[k - 1][rows : rows + tall, :] = part.astype(BF16)
            sent[k - 1][rows + tall :, :] = gain


def join_sums(mine, got, out_total, gain, others):
    owners, rows, _ = mine.shape
    size = out_total.shape[0]
    tall = rows + size // owners
    extra = gain.shape[0]
    return pl.pallas_call(
        functools.partial(join_kernel, owners=owners),
        out_shape=[shaped((tall, PAIR), F32), shaped((extra, PAIR), BF16)]
        + [shaped((tall + extra, PAIR), BF16)] * (owners - 1),
        in_specs=[VMEM] * (4 + len(others)),
        out_specs=[VMEM] * (owners + 1),
        compiler_params=params(24),
        cost_estimate=cost(owners * tall * PAIR * 4, owners * tall * PAIR * 10),
    )(mine, got, out_total, gain, *others)


def dense_out_kernel(ids_ref, near_ref, *refs, counts, s, n, owners, pairs, width):
    far = refs[: sum(counts)]
    w_ref = refs[sum(counts)]
    out_ref, dense_ref, sum_ref, held_ref, sems = refs[-5:]
    group = pairs * PAIR
    rows = out_ref.shape[0]
    tall = held_ref.shape[2]
    step = pl.program_id(0)

    def copies(k):
        found = []
        low, high = (k - 1) * tall, k * tall
        for r in range(n):
            if k == 0:
                source, target = near_ref.at[ids_ref[0] ^ r], held_ref.at[0, r]
                found.append(pltpu.make_async_copy(source, target, sems.at[0, r, 0]))
                continue
            begin = 0
            first = sum(counts[:r])
            for i, part in enumerate(far[first : first + counts[r]]):
                end = begin + part.shape[0]
                lo, hi = max(low, begin), min(high, end)
                if lo < hi:
                    source = part.at[pl.ds(lo - begin, hi - lo)]
                    target = held_ref.at[k % 2, r, pl.ds(lo - low, hi - lo)]
                    found.append(pltpu.make_async_copy(source, target, sems.at[k % 2, r, i]))
                begin = end
        return found

    @pl.when(step == 0)
    def _():
        for copy in copies(0):
            copy.start()

    for k in range(owners):

        @pl.when(step == k)
        def _():
            if k + 1 < owners:
                for copy in copies(k + 1):
                    copy.start()
            for copy in copies(k):
                copy.wait()

    slot = lax.rem(step, 2)
    out_rows = group // owners
    blocks = width // (2 * PAIR)
    for r in range(n):
        g = ids_ref[0] ^ r
        for part in range(3):
            for p in range(pairs):
                to = pl.multiple_of(part * width + g * group + p * PAIR, PAIR)
                at = (part * pairs + p) * rows
                out_ref[:, pl.ds(to, PAIR)] = held_ref[slot, r, at : at + rows, :].astype(F32)
        row = g * group + (ids_ref[1] ^ step) * out_rows
        row_at = pl.ds(pl.multiple_of(row, out_rows), out_rows)
        for b in range(blocks):
            at = 3 * pairs * rows + b * out_rows
            dense_ref[row_at, b * PAIR : (b + 1) * PAIR] = held_ref[
                slot, r, at : at + out_rows, :
            ].astype(F32)
    total = None
    for at in range(0, 3 * width, PAIR):
        term = out_ref[:, at : at + PAIR] * w_ref[:, at : at + PAIR].astype(F32)
        total = term if total is None else total + term
    sum_ref[...] = total


def dense_out(ids, near, far, w_qkv, s, owners, before=()):
    width = w_qkv.shape[0]
    n, tall, _ = near.shape
    rows = width // (2 * owners)
    anywhere = pl.BlockSpec(memory_space=pl.ANY)
    counts = [len(parts) for parts in far]
    parts = [part for line in far for part in line]

    def place(k, ids_ref):
        return ((ids_ref[2] ^ s) * owners + (ids_ref[1] ^ k), 0)

    return pl.pallas_call(
        functools.partial(
            dense_out_kernel,
            counts=counts,
            s=s,
            n=n,
            owners=owners,
            pairs=width // n // PAIR,
            width=width,
        ),
        out_shape=(
            shaped((width, 3 * width), F32),
            shaped((width, width), F32),
            shaped((width, PAIR), F32),
        ),
        grid_spec=pltpu.PrefetchScalarGridSpec(
            num_scalar_prefetch=1,
            grid=(owners,),
            in_specs=[anywhere] * (1 + len(parts))
            + [pl.BlockSpec((rows, 3 * width), place)]
            + [anywhere] * len(before),
            out_specs=(
                pl.BlockSpec((rows, 3 * width), place),
                pl.BlockSpec((width, width // 2), lambda k, ids_ref: (0, ids_ref[2] ^ s)),
                pl.BlockSpec((rows, PAIR), place),
            ),
            scratch_shapes=[
                pltpu.VMEM((2, n, tall, PAIR), BF16),
                pltpu.SemaphoreType.DMA((2, n, 2)),
            ],
        ),
        input_output_aliases={3 + len(parts) + i: i for i in range(len(before))},
        compiler_params=params(40),
        cost_estimate=cost(3 * width * width, 16 * width * width),
    )(ids, near, *parts, w_qkv, *before)


def back_kernel(d_ref, w_ref, x_ref, inv_ref, gain_ref, grad_ref, out_ref):
    n, _, _, group = d_ref.shape
    width = x_ref.shape[1]
    out_ref[...] = jnp.zeros_like(out_ref)

    @pl.loop(0, n)
    def _(g):
        for part in range(3):
            at = pl.ds(pl.multiple_of(part * width + g * group, group), group)
            out_ref[...] += matmul_nt(d_ref[g, part], w_ref[:, at])

    x = x_ref[...].astype(F32)
    inverse = inv_ref[...]
    scaled = out_ref[...] * gain_ref[...]
    inner = jnp.mean(scaled * x, axis=-1, keepdims=True)
    out_ref[...] = grad_ref[...] + inverse * scaled - x * (inverse**3 * inner)


def back_to_tokens(d, w_qkv, x, inverse, gain, grad_hidden):
    rows, width = x.shape
    return pl.pallas_call(
        back_kernel,
        out_shape=shaped((rows, width), F32),
        in_specs=[VMEM] * 6,
        out_specs=VMEM,
        compiler_params=params(32),
        cost_estimate=cost(6 * rows * width * width, 10 * width * width),
    )(d, w_qkv, x, inverse, gain, grad_hidden)


def on_device(
    tokens,
    out_grad,
    token_ids,
    hash_table,
    doc_lengths,
    w_qkv,
    w_out,
    gain_attn,
    gain_ffn,
    expert_in,
    expert_out,
):
    rows = tokens.shape[1]
    width = tokens.shape[2]
    n = lax.axis_size("ctx")
    owners = lax.axis_size("expert")
    rank = lax.axis_index("ctx")
    z = lax.axis_index("expert")
    core = lax.axis_index("dp")
    group = width // n
    pairs = group // PAIR
    length = n * rows
    ids = jnp.stack([rank, z, core]).astype(jnp.int32)

    inputs_low = tokens[0]

    capacity = rows * 5 // (4 * owners)
    slots = owners * capacity
    chosen = jnp.take(hash_table, token_ids[0], axis=0)
    order = jnp.arange(rows, dtype=jnp.int32)
    ahead = (chosen[:, None] == chosen[None, :]) & (order[None, :] < order[:, None])
    slot = jnp.sum(ahead.astype(jnp.int32), axis=1)
    code = (chosen ^ z) * capacity + slot
    picks = (jnp.arange(slots, dtype=jnp.int32)[:, None] == code[None, :]).astype(BF16)
    spots = jnp.arange(slots, dtype=jnp.int32).reshape(owners, 1, capacity)
    places = (code[None, :, None] == spots).astype(BF16)

    def send_rows(matrix):
        far = {}
        for k in list(range(owners // 2, owners)) + list(range(1, owners // 2)):
            far[k] = swap(matrix[k * capacity : (k + 1) * capacity], "expert", k)
        return [matrix[:capacity]] + [far[k] for k in range(1, owners)]

    def spread(piece, before=()):
        line = after(jnp.concatenate([piece, swap(piece, "ctx", 1)], axis=0), *before)
        return jnp.concatenate([line, swap(line, "dp", 1)], axis=0)

    upstream = out_grad[0]
    w_in, w_o = expert_in[0], expert_out[0]
    units = w_in.shape[1]
    top = width * 3 // 4
    upper = w_in[:top]
    up_rows = matmul(picks, upstream).astype(BF16)
    up_arrived = send_rows(up_rows)
    late_low = after(inputs_low, up_rows)
    blocks = [inputs_low] + [
        swap(inputs_low if r & (r - 1) == 0 else late_low, "ctx", r) for r in range(1, n)
    ]
    chunks = [list(range(0, owners // 2)), list(range(owners // 2, owners))]

    doc_ends = jnp.cumsum(doc_lengths[0])
    spots = jnp.arange(length, dtype=jnp.int32)
    later = doc_ends[:, None] > spots[None, :]
    ends = jnp.min(jnp.where(later, doc_ends[:, None], length), axis=0)[None, :].astype(jnp.int32)
    starts = jnp.max(jnp.where(later, 0, doc_ends[:, None]), axis=0)[None, :].astype(jnp.int32)
    normed, inverse_one, q_own, k_own, v_own, mixed_own, att, tot = attend_forward(
        ids, ends, gain_attn[None, :], blocks, w_qkv, n
    )

    rest = jnp.concatenate(
        [w_in[top:]] + [w_o[:, at : at + units] for at in range(0, width, units)], axis=0
    )
    first = after(upper, *blocks[1:])
    firsts = [swap(first, "ctx", m << 1) for m in range(1, n // 2)]
    mixed_own = after(mixed_own, firsts)
    up_line = after(jnp.concatenate(up_arrived, axis=0), mixed_own)
    up_line = jnp.concatenate([up_line[None], swap(up_line, "ctx", 1)[None]], axis=0)
    up_all = jnp.concatenate([up_line[None], swap(up_line, "dp", 1)[None]], axis=0)
    up_chunks = [
        up_all[:, :, c[0] * capacity : (c[-1] + 1) * capacity].reshape(-1, width) for c in chunks
    ]

    mixed_sent = [lax.dynamic_slice_in_dim(mixed_own, (rank ^ r) * rows, rows, 0) for r in range(n)]
    mixed_parts = [mixed_sent[0]] + [swap(mixed_sent[r], "ctx", r) for r in range(1, n)]
    rest = after(rest, mixed_parts)
    rests = [swap(rest, "ctx", m << 1) for m in range(1, n // 2)]
    hidden, inverse_two, row_sent = middle(
        ids, mixed_parts, w_out, inputs_low, gain_ffn[None, :], picks
    )

    near, far = chunks
    arrived = {0: row_sent[:capacity]}
    for k in near[1:] + far:
        arrived[k] = swap(row_sent[k * capacity : (k + 1) * capacity], "expert", k)
    near_rows = jnp.concatenate([arrived[k] for k in near], axis=0)
    far_rows = after(jnp.concatenate([arrived[k] for k in far], axis=0), near_rows)
    row_chunks = [spread(near_rows), spread(far_rows, rests)]
    sizes = [units] * (n // 2)
    acts = []
    grad_pres = []
    far_back = {}
    x_sent = []
    for c, row_chunk, up_chunk in list(zip(chunks, row_chunks, up_chunks))[::-1]:
        if acts:
            row_chunk = after(row_chunk, theirs)
        mine, theirs, act, grad_pre = expert_rows(
            row_chunk, up_chunk, w_in, w_o, firsts, rests
        )
        acts.append(act)
        grad_pres.append(grad_pre)
        line = mine.astype(F32) + swap(theirs, "dp", 1).astype(F32)
        half = line.shape[0] // 2
        x_sent.append(line[half:].astype(BF16))
        own = (line[:half] + swap(x_sent[-1], "ctx", 1).astype(F32)).astype(BF16)
        for i, k in reversed(list(enumerate(c))):
            piece = own[i * capacity : (i + 1) * capacity]
            far_back[k] = piece if k == 0 else swap(piece, "expert", k)
    back = [far_back[k] for k in range(owners)]
    acts, grad_pres = acts[::-1], grad_pres[::-1]
    last_own = own

    grads_out = weight_grads_out(after(acts, x_sent[0]), up_chunks, sizes)

    def others(grads):
        return [swap(grads[i], "ctx", i << 1) for i in range(1, len(grads))]

    out_others = others(grads_out)
    made, made_other = produce(
        after(acts, x_sent[1]), w_o, rests, [len(c) * capacity for c in chunks]
    )
    grads_in = weight_grads(row_chunks, after(grad_pres, x_sent[1]), sizes)
    back = after(back, made, grads_in)
    made_other = swap(made_other, "dp", 1)

    grad_hidden, grad_parts, mine, theirs = turn(
        ids, back, mixed_parts, places, hidden, upstream, inverse_two, gain_ffn[None, :], w_out
    )
    grad_parts = after(grad_parts, out_others)
    grad_att_own = jnp.concatenate(
        [grad_parts[0]] + [swap(grad_parts[r], "ctx", r) for r in range(1, n)], axis=0
    )

    def add_others(own, parts):
        for part in parts:
            own = own + part.astype(F32)
        return own

    cols = width // PAIR
    size = mine.shape[0]
    got = swap(theirs, "dp", 1)
    gain_low = (theirs[size:].astype(F32) + got[size:].astype(F32)).astype(BF16)
    total = mine + got[:size].astype(F32)
    piece = size // n
    out_sent = [
        jnp.concatenate([total[r * piece : (r + 1) * piece].astype(BF16), gain_low], axis=0)
        for r in range(1, n)
    ]
    out_sent = after(out_sent, grad_att_own)
    out_got = [swap(out_sent[r - 1], "ctx", r) for r in range(1, n)]

    held = after(grad_att_own, out_sent)
    d_own, mine, theirs = attend_backward(
        ids, starts, normed, q_own, k_own, v_own, att, tot, held, n, owners
    )
    d_own, theirs = after((d_own, theirs), out_got)
    d_pieces = exchange(d_own, "ctx")
    in_others = others(after(grads_in, d_pieces))
    made_line = made.astype(F32) + after(made_other, d_pieces).astype(F32)
    sent = made_line[1].astype(BF16)
    made_own = (made_line[0] + swap(sent, "ctx", 1).astype(F32)).astype(BF16)
    order = list(range(owners // 2, owners)) + list(range(1, owners // 2))
    own, gain_low, *messages = join_sums(
        mine, swap(theirs, "dp", 1), total[: total.shape[0] // n], gain_low, out_got
    )
    tall = own.shape[0]
    got = {k: swap(messages[k - 1], "expert", k) for k in order}
    piece = own
    gains = [gain_low.astype(F32)]
    for k in range(owners - 1, 0, -1):
        piece = piece + got[k][:tall].astype(F32)
    for k in range(1, owners):
        gains.append(got[k][tall:].astype(F32))
    while len(gains) > 1:
        gains = [gains[i] + gains[i + 1] for i in range(0, len(gains), 2)]
    grad_gain_ffn = gains[0][:cols].reshape(width)
    piece = piece.astype(BF16)
    arrived = {k: swap(piece, "expert", k) for k in order}
    near_lines = spread_to(piece, "ctx")
    line = jnp.concatenate([arrived[k] for k in range(1, owners)], axis=0)
    line = after(line, in_others, made_own, near_lines)
    if n == 4:
        half = line.shape[0] // 2
        one, two = swap(line, "ctx", 1), swap(line, "ctx", 2)
        sent = (one[:half], two[half:])
        last = [swap(sent[0], "ctx", 2), swap(sent[1], "ctx", 1)]
        far_lines = [[line], [one], [two], last]
        in_others, out_others, d_pieces = after((in_others, out_others, d_pieces), sent)
    else:
        far_lines = [[line]] + [[swap(line, "ctx", r)] for r in range(1, n)]
    grad_inputs = back_to_tokens(
        d_pieces,
        w_qkv,
        inputs_low,
        inverse_one,
        gain_attn[None, :],
        grad_hidden,
    )
    grad_expert_out = add_others(grads_out[0], out_others)
    grad_expert_in = add_others(grads_in[0], in_others)
    returned = jnp.concatenate(send_rows(after(made_own, line)), axis=0)
    block_out = (
        hidden + matmul(places.transpose(1, 0, 2).reshape(rows, slots), returned)
    ).astype(BF16)
    near_other = swap(near_lines, "dp", 1)
    far_lines[n - 1] = after(
        far_lines[n - 1], block_out, grad_inputs, grad_expert_out, grad_expert_in, near_other
    )
    first = dense_out(ids, near_lines, far_lines, w_qkv, 0, owners)
    far_other = [[swap(part, "dp", 1) for part in parts] for parts in far_lines]
    grad_w_qkv, grad_w_out, gain_sums = dense_out(
        ids, near_other, far_other, w_qkv, 1, owners, first
    )
    grad_gain_attn = jnp.sum(gain_sums, axis=1) / gain_attn

    return (
        block_out[None],
        grad_inputs[None],
        grad_w_qkv,
        grad_w_out,
        grad_gain_attn,
        grad_gain_ffn,
        grad_expert_in[None],
        grad_expert_out[None],
    )


def solution(mesh):
    rows = P(("expert", "dp"), "ctx", None)
    placed = (
        rows,
        rows,
        P(("expert", "dp"), "ctx"),
        P(),
        P(("expert", "dp"), None),
        P(),
        P(),
        P(),
        P(),
        P("expert", None, ("ctx", "dp")),
        P("expert", ("ctx", "dp"), None),
    )
    return jax.shard_map(
        on_device,
        mesh=mesh,
        in_specs=placed,
        out_specs=(
            rows,
            rows,
            P(),
            P(),
            P(),
            P(),
            P("expert", None, ("ctx", "dp")),
            P("expert", ("ctx", "dp"), None),
        ),
        check_vma=False,
    )
```

profile of v0, /device:TPU:0, one launch (start us, length us, event | category | flops | bytes accessed | tf_op | source)
XLA Modules:
  0.0 294.5 jit_solution(4564616623689846643)
XLA Ops:
  10.7 4.0 %collective-permute-start.17 = (bf16[80,1024]{1,0:T(8,128)(2,1)}, bf16[80,1024]{1,0:T(8,128)(2,1)}, u32[]{:S(2)}, u32[]{:S(2)}) collective-permute-start(bf16[80,1024]{1,0:T(8,128)(2,1)} %get-tuple-element.180), channel_id=1, source_target_pairs={{0,24},{8,16},{16,8},{24,0},{1,25},{9,17},{17,9},{25,1},{2,26},{10... | collective-permute-start | bytes 491528 | tf_op jit(solution)/shard_map/ppermute | solution.py:24
  18.9 9.5 %collective-permute-done.2.refs_3_ = bf16[256,1024]{1,0:T(8,128)(2,1)S(1)} collective-permute-done((bf16[256,1024]{1,0:T(8,128)(2,1)S(1)}, bf16[256,1024]{1,0:T(8,128)(2,1)S(1)}, u32[]{:S(2)}, u32[]{:S(2)}) %collective-permute-start.2) | collective-permute-done | bytes 524320 | tf_op jit(solution)/shard_map/ppermute | solution.py:24
  34.3 10.6 %shard_map.170 = (bf16[1024,1024]{1,0:T(8,128)(2,1)}, f32[256,1]{1,0:T(8,128)S(1)}, bf16[1024,256]{1,0:T(8,128)(2,1)S(1)}, bf16[1024,256]{1,0:T(8,128)(2,1)S(1)}...) custom-call(s32[3]{0:T(128)S(1)} %pad_add_fusion.ids_ref, ...), custom_call_target="tpu_custom_call" | custom-call | flops 738197504 | bytes 2490368 | tf_op jit(solution)/shard_map/pallas_call | solution.py:140
  64.4 4.4 %collective-permute-done.18 = bf16[320,1024]{1,0:T(8,128)(2,1)S(1)} collective-permute-done((bf16[320,1024]{1,0:T(8,128)(2,1)S(1)}, bf16[320,1024]{1,0:T(8,128)(2,1)S(1)}, u32[]{:S(2)}, u32[]{:S(2)}) %collective-permute-start.18) | collective-permute-done | bytes 655392 | tf_op jit(solution)/shard_map/ppermute | solution.py:24
  71.6 4.1 %collective-permute-done.7 = bf16[80,1024]{1,0:T(8,128)(2,1)S(1)} collective-permute-done((bf16[80,1024]{1,0:T(8,128)(2,1)S(1)}, bf16[80,1024]{1,0:T(8,128)(2,1)S(1)}, u32[]{:S(2)}, u32[]{:S(2)}) %collective-permute-start.7) | collective-permute-done | bytes 163872 | tf_op jit(solution)/shard_map/ppermute | solution.py:24
  77.8 8.6 %collective-permute-done.12 = bf16[160,1024]{1,0:T(8,128)(2,1)S(1)} collective-permute-done((bf16[160,1024]{1,0:T(8,128)(2,1)S(1)}, bf16[160,1024]{1,0:T(8,128)(2,1)S(1)}, u32[]{:S(2)}, u32[]{:S(2)}) %collective-permute-start.12) | collective-permute-done | bytes 327712 | tf_op jit(solution)/shard_map/ppermute | solution.py:24
  86.6 5.5 %collective-permute-done.8 = bf16[160,1024]{1,0:T(8,128)(2,1)S(1)} collective-permute-done((bf16[160,1024]{1,0:T(8,128)(2,1)S(1)}, bf16[160,1024]{1,0:T(8,128)(2,1)S(1)}, u32[]{:S(2)}, u32[]{:S(2)}) %collective-permute-start.8) | collective-permute-done | bytes 327712 | tf_op jit(solution)/shard_map/ppermute | solution.py:24
  92.6 5.1 %shard_map.172 = (bf16[320,1024]{1,0:T(8,128)(2,1)S(1)}, bf16[320,1024]{1,0:T(8,128)(2,1)S(1)}, bf16[640,1024]{1,0:T(8,128)(2,1)S(1)}, bf16[640,1024]{1,0:T(8,128)(2,1)S(1)}) custom-call(bf16[640,1024]{1,0:T(8,128)(2,1)S(1)} %constant_dynamic-update-slice_fusion.refs_0_.refs_1_, bf16[640,1024]{1,0:T(8,128)(2,1)S(1)} %bitcast.66, ...), custom_call_target="tpu_custom_call" | custom-call | flops 1006632960 | bytes 2359296 | tf_op jit(solution)/shard_map/pallas_call | solution.py:254
  98.4 5.3 %shard_map.173 = (bf16[320,1024]{1,0:T(8,128)(2,1)S(1)}, bf16[320,1024]{1,0:T(8,128)(2,1)S(1)}, bf16[640,1024]{1,0:T(8,128)(2,1)S(1)}, bf16[640,1024]{1,0:T(8,128)(2,1)S(1)}) custom-call(bf16[640,1024]{1,0:T(8,128)(2,1)S(1)} %pad_maximum_fusion.1.refs_0_, bf16[640,1024]{1,0:T(8,128)(2,1)S(1)} %bitcast.64, bf16[1024,512]{1,0:T(8,128)(2,1)S(1)} %bitcast.69, ...), custom_call_target="tpu_custom_call" | custom-call | flops 1006632960 | bytes 2359296 | tf_op jit(solution)/shard_map/pallas_call | solution.py:254
  107.7 4.6 %shard_map.177 = (f32[512,1024]{1,0:T(8,128)S(1)}, bf16[512,1024]{1,0:T(8,128)(2,1)S(1)}) custom-call(bf16[640,1024]{1,0:T(8,128)(2,1)S(1)} %get-tuple-element.124.refs_0_, bf16[640,1024]{1,0:T(8,128)(2,1)S(1)} %get-tuple-element.125.refs_1_, bf16[640,1024]{1,0:T(8,128)(2,1)S(1)} %bitcast.65, bf16[640,1024]{1,0:T(8,128)(2,1)S(1)} %bitcast.67), custom_call_target="tpu_custom_call" | custom-call | flops 671088640 | bytes 2097152 | tf_op jit(solution)/shard_map/pallas_call | solution.py:400
  122.9 5.1 %shard_map.175 = (f32[1024,512]{1,0:T(8,128)S(1)}, bf16[1024,512]{1,0:T(8,128)(2,1)}) custom-call(bf16[640,1024]{1,0:T(8,128)(2,1)S(1)} %pad_maximum_fusion.1.refs_0_, bf16[640,1024]{1,0:T(8,128)(2,1)S(1)} %constant_dynamic-update-slice_fusion.refs_0_.refs_1_, bf16[640,1024]{1,0:T(8,128)(2,1)S(1)} %get-tuple-element.114.refs_2_, ...), custom_call_target="tpu_custom_call" | custom-call | flops 671088640 | bytes 2097152 | tf_op jit(solution)/shard_map/pallas_call | solution.py:355
  129.4 4.9 %shard_map.174 = (bf16[2,320,1024]{2,1,0:T(8,128)(2,1)S(1)}, bf16[2,320,1024]{2,1,0:T(8,128)(2,1)}) custom-call(bf16[640,1024]{1,0:T(8,128)(2,1)S(1)} %get-tuple-element.124.refs_0_, bf16[640,1024]{1,0:T(8,128)(2,1)S(1)} %get-tuple-element.125.refs_1_, bf16[512,1024]{1,0:T(8,128)(2,1)S(1)} %bitcast.63, ...), custom_call_target="tpu_custom_call" | custom-call | flops 671088640 | bytes 1835008 | tf_op jit(solution)/shard_map/pallas_call | solution.py:448
  135.3 4.2 %shard_map.176 = (f32[256,1024]{1,0:T(8,128)S(1)}, bf16[4,256,256]{2,1,0:T(8,128)(2,1)S(1)}, f32[4096,128]{1,0:T(8,128)S(1)}, bf16[4112,128]{1,0:T(8,128)(2,1)S(1)}) custom-call(s32[3]{0:T(128)S(1)} %pad_add_fusion.ids_ref, bf16[80,1024]{1,0:T(8,128)(2,1)S(1)} %get-tuple-element.118.refs_0_, bf16[80,1024]{1,0:T(8,128)(2,1)S(1)} %collective-permute-done.23.refs_1_, ...), custom_call_target="tpu_custom_call" | custom-call | flops 335544320 | bytes 2621440 | tf_op jit(solution)/shard_map/pallas_call | solution.py:321
  143.2 3.8 %collective-permute-done.31 = bf16[256,256]{1,0:T(8,128)(2,1)S(1)} collective-permute-done((bf16[256,256]{1,0:T(8,128)(2,1)S(1)}, bf16[256,256]{1,0:T(8,128)(2,1)S(1)}, u32[]{:S(2)}, u32[]{:S(2)}) %collective-permute-start.31) | collective-permute-done | bytes 131104 | tf_op jit(solution)/shard_map/ppermute | solution.py:24
  154.8 16.8 %shard_map.178 = (bf16[4,3,256,256]{3,2,1,0:T(8,128)(2,1)}, f32[4,768,128]{2,1,0:T(8,128)}, bf16[4,768,128]{2,1,0:T(8,128)(2,1)S(1)}) custom-call(s32[3]{0:T(128)S(1)} %pad_add_fusion.ids_ref, s32[1,1024]{1,0:T(1,128)S(1)} %bitcast.81, bf16[1024,1024]{1,0:T(8,128)(2,1)} %get-tuple-element.105.normed_ref, bf16[1024,256]{1,0:T(8,128)(2,1)S(1)} %copy-done.23, ...), custom_call_target="tpu_custom_call" | custom-call | flops 1241513984 | bytes 2686976 | tf_op jit(solution)/shard_map/pallas_call | solution.py:558
  185.5 10.6 %all-to-all-done.d_ref = bf16[4,3,256,256]{3,2,1,0:T(8,128)(2,1)S(1)} async-done(((bf16[4,3,256,256]{3,2,1,0:T(8,128)(2,1)}), bf16[4,3,256,256]{3,2,1,0:T(8,128)(2,1)S(1)}, u32[]{:S(2)}, u32[]{:S(2)}) %all-to-all-start) | async-done | bytes 1572896 | tf_op jit(solution)/shard_map/all_to_all | solution.py:28
  202.0 6.0 %collective-permute-done.39 = bf16[1040,128]{1,0:T(8,128)(2,1)S(1)} collective-permute-done((bf16[1040,128]{1,0:T(8,128)(2,1)}, bf16[1040,128]{1,0:T(8,128)(2,1)S(1)}, u32[]{:S(2)}, u32[]{:S(2)}) %collective-permute-start.39) | collective-permute-done | bytes 266272 | tf_op jit(solution)/shard_map/ppermute | solution.py:24
  214.7 4.5 %all-to-all-start.1 = ((bf16[4,1024,128]{2,1,0:T(8,128)(2,1)}), bf16[4,1024,128]{2,1,0:T(8,128)(2,1)}, u32[]{:S(2)}, u32[]{:S(2)}) async-start(bf16[4,1024,128]{2,1,0:T(8,128)(2,1)} %broadcast_in_dim.95), calls=%async_computation.1 | async-start | bytes 2097152 | tf_op jit(solution)/shard_map/all_to_all | solution.py:28
  220.3 12.9 %collective-permute-done.42 = bf16[1024,128]{1,0:T(8,128)(2,1)S(1)} collective-permute-done((bf16[1024,128]{1,0:T(8,128)(2,1)S(1)}, bf16[1024,128]{1,0:T(8,128)(2,1)S(1)}, u32[]{:S(2)}, u32[]{:S(2)}) %collective-permute-start.42) | collective-permute-done | bytes 262176 | tf_op jit(solution)/shard_map/ppermute | solution.py:24
  244.1 6.4 %collective-permute-done.47 = bf16[80,1024]{1,0:T(8,128)(2,1)S(1)} collective-permute-done((bf16[80,1024]{1,0:T(8,128)(2,1)S(1)}, bf16[80,1024]{1,0:T(8,128)(2,1)S(1)}, u32[]{:S(2)}, u32[]{:S(2)}) %collective-permute-start.47) | collective-permute-done | bytes 163872 | tf_op jit(solution)/shard_map/ppermute | solution.py:24
  251.2 6.2 %collective-permute-start.45 = (bf16[80,1024]{1,0:T(8,128)(2,1)}, bf16[80,1024]{1,0:T(8,128)(2,1)}, u32[]{:S(2)}, u32[]{:S(2)}) collective-permute-start(bf16[80,1024]{1,0:T(8,128)(2,1)} %get-tuple-element.178), channel_id=1, source_target_pairs={{0,8},{8,0},{16,24},{24,16},{1,9},{9,1},{17,25},{25,17},{2,10},{10... | collective-permute-start | bytes 491528 | tf_op jit(solution)/shard_map/ppermute | solution.py:24
  273.2 4.0 %shard_map.180 = f32[256,1024]{1,0:T(8,128)} custom-call(bf16[4,3,256,256]{3,2,1,0:T(8,128)(2,1)S(1)} %copy-done.6, bf16[1024,3072]{1,0:T(8,128)(2,1)S(1)} %bitcast.57, bf16[256,1024]{1,0:T(8,128)(2,1)S(1)} %bitcast.75, f32[256,1]{1,0:T(8,128)S(1)} %copy-done.35, f32[1,1024]{1,0:T(1,128)S(1)} %bitcast.78, f32[256,1024]{1,0:T(8,128)S(1)} %copy-done.17), custom_call_target="tpu_custom_call" | custom-call | flops 402653184 | bytes 2621440 | tf_op jit(solution)/shard_map/pallas_call | solution.py:764
  280.7 6.6 %shard_map.181 = (f32[1024,3072]{1,0:T(8,128)}, f32[1024,1024]{1,0:T(8,128)}, f32[1024,128]{1,0:T(8,128)S(1)}) custom-call(s32[3]{0:T(128)S(1)} %pad_add_fusion.ids_ref, bf16[4,1024,128]{2,1,0:T(8,128)(2,1)} %all-to-all-done.1.near_ref, bf16[3072,128]{1,0:T(8,128)(2,1)S(1)} %pad_maximum_fusion.4.refs_0_, bf16[3072,128]{1,0:T(8,128)(2,1)} %collective-permute-done.48.refs_1_, ...), custom_call_target="tpu_custom_call" | custom-call | flops 786432 | bytes 4194304 | tf_op jit(solution)/shard_map/pallas_call | solution.py:707
  287.5 6.2 %shard_map.182 = (f32[1024,3072]{1,0:T(8,128)}, f32[1024,1024]{1,0:T(8,128)}, f32[1024,128]{1,0:T(8,128)S(1)}) custom-call(s32[3]{0:T(128)S(1)} %pad_add_fusion.ids_ref, bf16[4,1024,128]{2,1,0:T(8,128)(2,1)} %collective-permute-done.50.near_ref, ...), custom_call_target="tpu_custom_call", output_to_operand_aliasing={{0}: (8, {}), {1}: (9, {}), {2}: (10, {})} | custom-call | flops 786432 | bytes 4194304 | tf_op jit(solution)/shard_map/pallas_call | solution.py:707
  (294 shorter events, 133.2 us)
Async XLA Ops:
  9.7 18.7 %collective-permute-start.2 = (bf16[256,1024]{1,0:T(8,128)(2,1)S(1)}, bf16[256,1024]{1,0:T(8,128)(2,1)S(1)}, u32[]{:S(2)}, u32[]{:S(2)}) collective-permute-start(bf16[256,1024]{1,0:T(8,128)(2,1)S(1)} %bitcast.72), channel_id=1, source_target_pairs={{0,6},{2,4},{4,2},{6,0},{1,7},{3,5},{5,3},{7,1},{8,14},{10,12},{12... | collective-permute-start | bytes 1572872 | tf_op jit(solution)/shard_map/ppermute | solution.py:24
  10.7 22.2 %collective-permute-start.17 = (bf16[80,1024]{1,0:T(8,128)(2,1)}, bf16[80,1024]{1,0:T(8,128)(2,1)}, u32[]{:S(2)}, u32[]{:S(2)}) collective-permute-start(bf16[80,1024]{1,0:T(8,128)(2,1)} %get-tuple-element.180), channel_id=1, source_target_pairs={{0,24},{8,16},{16,8},{24,0},{1,25},{9,17},{17,9},{25,1},{2,26},{10... | collective-permute-start | bytes 491528 | tf_op jit(solution)/shard_map/ppermute | solution.py:24
  14.7 18.3 %collective-permute-start.16 = (bf16[80,1024]{1,0:T(8,128)(2,1)}, bf16[80,1024]{1,0:T(8,128)(2,1)}, u32[]{:S(2)}, u32[]{:S(2)}) collective-permute-start(bf16[80,1024]{1,0:T(8,128)(2,1)} %get-tuple-element.181), channel_id=1, source_target_pairs={{0,16},{8,24},{16,0},{24,8},{1,17},{9,25},{17,1},{25,9},{2,18},{10... | collective-permute-start | bytes 491528 | tf_op jit(solution)/shard_map/ppermute | solution.py:24
  29.1 18.7 %collective-permute-start.3 = (bf16[768,512]{1,0:T(8,128)(2,1)}, bf16[768,512]{1,0:T(8,128)(2,1)S(1)}, u32[]{:S(2)}, u32[]{:S(2)}) collective-permute-start(bf16[768,512]{1,0:T(8,128)(2,1)} %slice_bitcast_fusion.1), channel_id=1, source_target_pairs={{0,4},{2,6},{4,0},{6,2},{1,5},{3,7},{5,1},{7,3},{8,12},{10,14},{12... | collective-permute-start | bytes 2359304 | tf_op jit(solution)/shard_map/ppermute | solution.py:24
  58.0 28.5 %collective-permute-start.13 = (bf16[1280,512]{1,0:T(8,128)(2,1)S(1)}, bf16[1280,512]{1,0:T(8,128)(2,1)S(1)}, u32[]{:S(2)}, u32[]{:S(2)}) collective-permute-start(bf16[1280,512]{1,0:T(8,128)(2,1)S(1)} %pad_maximum_fusion.2), channel_id=1, source_target_pairs={{0,4},{2,6},{4,0},{6,2},{1,5},{3,7},{5,1},{7,3},{8,12},{10,14},{12... | collective-permute-start | bytes 3932168 | tf_op jit(solution)/shard_map/ppermute | solution.py:24
  69.0 23.3 %collective-permute-start.19 = (bf16[2,320,1024]{2,1,0:T(8,128)(2,1)S(1)}, bf16[2,320,1024]{2,1,0:T(8,128)(2,1)S(1)}, u32[]{:S(2)}, u32[]{:S(2)}) collective-permute-start(bf16[2,320,1024]{2,1,0:T(8,128)(2,1)S(1)} %get-tuple-element.168), channel_id=1, source_target_pairs={{0,1},{1,0},{2,3},{3,2},{4,5},{5,4},{6,7},{7,6},{8,9},{9,8},{10,11... | collective-permute-start | bytes 3932168 | tf_op jit(solution)/shard_map/ppermute | solution.py:24
  112.2 27.3 %collective-permute-start.28 = (bf16[512,1024]{1,0:T(8,128)(2,1)S(1)}, bf16[512,1024]{1,0:T(8,128)(2,1)S(1)}, u32[]{:S(2)}, u32[]{:S(2)}) collective-permute-start(bf16[512,1024]{1,0:T(8,128)(2,1)S(1)} %get-tuple-element.126), channel_id=1, source_target_pairs={{0,4},{2,6},{4,0},{6,2},{1,5},{3,7},{5,1},{7,3},{8,12},{10,14},{12... | collective-permute-start | bytes 3145736 | tf_op jit(solution)/shard_map/ppermute | solution.py:24
  114.7 19.5 %collective-permute-start.27 = (bf16[80,1024]{1,0:T(8,128)(2,1)S(1)}, bf16[80,1024]{1,0:T(8,128)(2,1)S(1)}, u32[]{:S(2)}, u32[]{:S(2)}) collective-permute-start(bf16[80,1024]{1,0:T(8,128)(2,1)S(1)} %get-tuple-element.195), channel_id=1, source_target_pairs={{0,24},{8,16},{16,8},{24,0},{1,25},{9,17},{17,9},{25,1},{2,26},{10... | collective-permute-start | bytes 491528 | tf_op jit(solution)/shard_map/ppermute | solution.py:24
  151.2 20.4 %collective-permute-start.33 = (bf16[1040,128]{1,0:T(8,128)(2,1)S(1)}, bf16[1040,128]{1,0:T(8,128)(2,1)S(1)}, u32[]{:S(2)}, u32[]{:S(2)}) collective-permute-start(bf16[1040,128]{1,0:T(8,128)(2,1)S(1)} %get-tuple-element.130), channel_id=1, source_target_pairs={{0,2},{2,0},{4,6},{6,4},{1,3},{3,1},{5,7},{7,5},{8,10},{10,8},{12,... | collective-permute-start | bytes 798728 | tf_op jit(solution)/shard_map/ppermute | solution.py:24
  152.7 18.9 %collective-permute-start.34 = (bf16[1040,128]{1,0:T(8,128)(2,1)S(1)}, bf16[1040,128]{1,0:T(8,128)(2,1)S(1)}, u32[]{:S(2)}, u32[]{:S(2)}) collective-permute-start(bf16[1040,128]{1,0:T(8,128)(2,1)S(1)} %get-tuple-element.131), channel_id=1, source_target_pairs={{0,4},{2,6},{4,0},{6,2},{1,5},{3,7},{5,1},{7,3},{8,12},{10,14},{12... | collective-permute-start | bytes 798728 | tf_op jit(solution)/shard_map/ppermute | solution.py:24
  154.7 41.4 %collective-permute-start.21 = (bf16[2,320,1024]{2,1,0:T(8,128)(2,1)}, bf16[2,320,1024]{2,1,0:T(8,128)(2,1)}, u32[]{:S(2)}, u32[]{:S(2)}) collective-permute-start(bf16[2,320,1024]{2,1,0:T(8,128)(2,1)} %get-tuple-element.104), channel_id=1, source_target_pairs={{0,1},{1,0},{2,3},{3,2},{4,5},{5,4},{6,7},{7,6},{8,9},{9,8},{10,11... | collective-permute-start | bytes 3932168 | tf_op jit(solution)/shard_map/ppermute | solution.py:24
  172.4 23.7 %all-to-all-start = ((bf16[4,3,256,256]{3,2,1,0:T(8,128)(2,1)}), bf16[4,3,256,256]{3,2,1,0:T(8,128)(2,1)S(1)}, u32[]{:S(2)}, u32[]{:S(2)}) async-start(bf16[4,3,256,256]{3,2,1,0:T(8,128)(2,1)} %get-tuple-element.136), calls=%async_computation | async-start | bytes 3145728 | tf_op jit(solution)/shard_map/all_to_all | solution.py:28
  181.1 20.9 %collective-permute-start.38 = (bf16[1040,128]{1,0:T(8,128)(2,1)}, bf16[1040,128]{1,0:T(8,128)(2,1)S(1)}, u32[]{:S(2)}, u32[]{:S(2)}) collective-permute-start(bf16[1040,128]{1,0:T(8,128)(2,1)} %get-tuple-element.141), channel_id=1, source_target_pairs={{0,24},{8,16},{16,8},{24,0},{1,25},{9,17},{17,9},{25,1},{2,26},{10... | collective-permute-start | bytes 798728 | tf_op jit(solution)/shard_map/ppermute | solution.py:24
  183.6 24.4 %collective-permute-start.39 = (bf16[1040,128]{1,0:T(8,128)(2,1)}, bf16[1040,128]{1,0:T(8,128)(2,1)S(1)}, u32[]{:S(2)}, u32[]{:S(2)}) collective-permute-start(bf16[1040,128]{1,0:T(8,128)(2,1)} %get-tuple-element.142), channel_id=1, source_target_pairs={{0,16},{8,24},{16,0},{24,8},{1,17},{9,25},{17,1},{25,9},{2,18},{10... | collective-permute-start | bytes 798728 | tf_op jit(solution)/shard_map/ppermute | solution.py:24
  183.7 24.2 %collective-permute-start.40 = (bf16[1040,128]{1,0:T(8,128)(2,1)}, bf16[1040,128]{1,0:T(8,128)(2,1)}, u32[]{:S(2)}, u32[]{:S(2)}) collective-permute-start(bf16[1040,128]{1,0:T(8,128)(2,1)} %get-tuple-element.143), channel_id=1, source_target_pairs={{0,8},{8,0},{16,24},{24,16},{1,9},{9,1},{17,25},{25,17},{2,10},{10... | collective-permute-start | bytes 798728 | tf_op jit(solution)/shard_map/ppermute | solution.py:24
  200.0 33.3 %collective-permute-start.36 = (bf16[320,1024]{1,0:T(8,128)(2,1)}, bf16[320,1024]{1,0:T(8,128)(2,1)}, u32[]{:S(2)}, u32[]{:S(2)}) collective-permute-start(bf16[320,1024]{1,0:T(8,128)(2,1)} %fusion.4), channel_id=1, source_target_pairs={{0,2},{2,0},{4,6},{6,4},{1,3},{3,1},{5,7},{7,5},{8,10},{10,8},{12,... | collective-permute-start | bytes 1966088 | tf_op jit(solution)/shard_map/ppermute | solution.py:24
  201.4 36.0 %collective-permute-start.44 = (bf16[1024,512]{1,0:T(8,128)(2,1)}, bf16[1024,512]{1,0:T(8,128)(2,1)}, u32[]{:S(2)}, u32[]{:S(2)}) collective-permute-start(bf16[1024,512]{1,0:T(8,128)(2,1)} %get-tuple-element.144), channel_id=1, source_target_pairs={{0,4},{2,6},{4,0},{6,2},{1,5},{3,7},{5,1},{7,3},{8,12},{10,14},{12... | collective-permute-start | bytes 3145736 | tf_op jit(solution)/shard_map/ppermute | solution.py:24
  211.9 21.3 %collective-permute-start.42 = (bf16[1024,128]{1,0:T(8,128)(2,1)S(1)}, bf16[1024,128]{1,0:T(8,128)(2,1)S(1)}, u32[]{:S(2)}, u32[]{:S(2)}) collective-permute-start(bf16[1024,128]{1,0:T(8,128)(2,1)S(1)} %add_convert_fusion), channel_id=1, source_target_pairs={{0,16},{8,24},{16,0},{24,8},{1,17},{9,25},{17,1},{25,9},{2,18},{10... | collective-permute-start | bytes 786440 | tf_op jit(solution)/shard_map/ppermute | solution.py:24
  211.9 21.3 %collective-permute-start.41 = (bf16[1024,128]{1,0:T(8,128)(2,1)S(1)}, bf16[1024,128]{1,0:T(8,128)(2,1)S(1)}, u32[]{:S(2)}, u32[]{:S(2)}) collective-permute-start(bf16[1024,128]{1,0:T(8,128)(2,1)S(1)} %add_convert_fusion), channel_id=1, source_target_pairs={{0,8},{8,0},{16,24},{24,16},{1,9},{9,1},{17,25},{25,17},{2,10},{10... | collective-permute-start | bytes 786440 | tf_op jit(solution)/shard_map/ppermute | solution.py:24
  214.7 22.7 %all-to-all-start.1 = ((bf16[4,1024,128]{2,1,0:T(8,128)(2,1)}), bf16[4,1024,128]{2,1,0:T(8,128)(2,1)}, u32[]{:S(2)}, u32[]{:S(2)}) async-start(bf16[4,1024,128]{2,1,0:T(8,128)(2,1)} %broadcast_in_dim.95), calls=%async_computation.1 | async-start | bytes 2097152 | tf_op jit(solution)/shard_map/all_to_all | solution.py:28
  237.5 35.2 %collective-permute-start.50 = (bf16[4,1024,128]{2,1,0:T(8,128)(2,1)}, bf16[4,1024,128]{2,1,0:T(8,128)(2,1)}, u32[]{:S(2)}, u32[]{:S(2)}) collective-permute-start(bf16[4,1024,128]{2,1,0:T(8,128)(2,1)} %all-to-all-done.1.near_ref), channel_id=1, source_target_pairs={{0,1},{1,0},{2,3},{3,2},{4,5},{5,4},{6,7},{7,6},{8,9},{9,8},{10,11... | collective-permute-start | bytes 3145736 | tf_op jit(solution)/shard_map/ppermute | solution.py:24
  237.5 28.1 %collective-permute-start.49 = (bf16[3072,128]{1,0:T(8,128)(2,1)S(1)}, bf16[3072,128]{1,0:T(8,128)(2,1)}, u32[]{:S(2)}, u32[]{:S(2)}) collective-permute-start(bf16[3072,128]{1,0:T(8,128)(2,1)S(1)} %pad_maximum_fusion.4.refs_0_), channel_id=1, source_target_pairs={{0,4},{2,6},{4,0},{6,2},{1,5},{3,7},{5,1},{7,3},{8,12},{10,14},{12... | collective-permute-start | bytes 2359304 | tf_op jit(solution)/shard_map/ppermute | solution.py:24
  238.0 29.1 %collective-permute-start.48 = (bf16[3072,128]{1,0:T(8,128)(2,1)S(1)}, bf16[3072,128]{1,0:T(8,128)(2,1)}, u32[]{:S(2)}, u32[]{:S(2)}) collective-permute-start(bf16[3072,128]{1,0:T(8,128)(2,1)S(1)} %pad_maximum_fusion.4.refs_0_), channel_id=1, source_target_pairs={{0,2},{2,0},{4,6},{6,4},{1,3},{3,1},{5,7},{7,5},{8,10},{10,8},{12,... | collective-permute-start | bytes 2359304 | tf_op jit(solution)/shard_map/ppermute | solution.py:24
  259.2 28.2 %collective-permute-start.51 = (bf16[3072,128]{1,0:T(8,128)(2,1)S(1)}, bf16[3072,128]{1,0:T(8,128)(2,1)S(1)}, u32[]{:S(2)}, u32[]{:S(2)}) collective-permute-start(bf16[3072,128]{1,0:T(8,128)(2,1)S(1)} %pad_maximum_fusion.4.refs_0_), channel_id=1, source_target_pairs={{0,1},{1,0},{2,3},{3,2},{4,5},{5,4},{6,7},{7,6},{8,9},{9,8},{10,11... | collective-permute-start | bytes 2359304 | tf_op jit(solution)/shard_map/ppermute | solution.py:24
  (95 other events, 874.4 us)
where the time goes:
time: 295 us; the launch traced here: 294 us
  waiting for transfers between devices  96.9 us (33%)
  Pallas kernels  75.9 us (26%)
  starting transfers between devices  75.5 us (26%)
  local copies, waits for them, and re-layouts  21.6 us (7%)
  other arithmetic  19.7 us (7%)
  matrix products  3.31 us (1%)
    ppermute x58, waiting for transfers between devices, swap(): return lax.ppermute(value, axis, [(i, i ^ bits) for i in range(size)])  84.8 us
    ppermute x58, starting transfers between devices, swap(): return lax.ppermute(value, axis, [(i, i ^ bits) for i in range(size)])  67.4 us
    pallas_call x1, Pallas kernels, attend_backward(): pl.pallas_call(functools.partial(backward_kernel, n=n, rows=rows, owners=...  16.8 us
    pallas_call x2, Pallas kernels, dense_out(): pl.pallas_call(functools.partial(dense_out_kernel, counts=counts, s=s, n=...  12.8 us
    all_to_all x2, waiting for transfers between devices, exchange(): return lax.all_to_all(value, axis, split_axis=0, concat_axis=0, tiled=True)  12.1 us
    pallas_call x1, Pallas kernels, attend_forward(): pl.pallas_call(functools.partial(forward_kernel, n=n, rows=rows), out_sha...  10.6 us
    pallas_call x2, Pallas kernels, expert_rows(): pl.pallas_call(functools.partial(expert_kernel, m=m), out_shape=[shaped((...  10.4 us
    all_to_all x2, starting transfers between devices, exchange(): return lax.all_to_all(value, axis, split_axis=0, concat_axis=0, tiled=True)  8.07 us
  transfers between devices with their start and end apart: 60, of which 28 were waited for; matrix products, arithmetic and copies ran while one was open for 12% of the time, Pallas kernels for 24%

commit v1 on v0

--- a/solution.py
+++ b/solution.py
@@ -847,7 +847,7 @@
     first = after(upper, *blocks[1:])
     firsts = [swap(first, "ctx", m << 1) for m in range(1, n // 2)]
     mixed_own = after(mixed_own, firsts)
-    up_line = after(jnp.concatenate(up_arrived, axis=0), mixed_own)
+    up_line = jnp.concatenate(after(up_arrived, mixed_own), axis=0)
     up_line = jnp.concatenate([up_line[None], swap(up_line, "ctx", 1)[None]], axis=0)
     up_all = jnp.concatenate([up_line[None], swap(up_line, "dp", 1)[None]], axis=0)
     up_chunks = [

time: 295 us -> 296 us (level)
    unnamed x115 -> x102, local copies, waits for them, and re-layouts: 7.97 us -> 7.83 us
  transfers between devices with their start and end apart: 60 -> 60, of which waited for: 28 -> 25; matrix products, arithmetic and copies ran while one was open for 12% -> 12% of each run, Pallas kernels for 24% -> 24%
where the time goes in v1:
time: 296 us; the launch traced here: 295 us
  waiting for transfers between devices  96.5 us (33%)
  starting transfers between devices  76.6 us (26%)
  Pallas kernels  76.1 us (26%)
  local copies, waits for them, and re-layouts  21.3 us (7%)
  other arithmetic  19.5 us (7%)
  matrix products  3.31 us (1%)
    ppermute x58, waiting for transfers between devices, swap(): return lax.ppermute(value, axis, [(i, i ^ bits) for i in range(size)])  84.4 us
    ppermute x58, starting transfers between devices, swap(): return lax.ppermute(value, axis, [(i, i ^ bits) for i in range(size)])  68.5 us
    pallas_call x1, Pallas kernels, attend_backward(): pl.pallas_call(functools.partial(backward_kernel, n=n, rows=rows, owners=...  16.8 us
    pallas_call x2, Pallas kernels, dense_out(): pl.pallas_call(functools.partial(dense_out_kernel, counts=counts, s=s, n=...  12.8 us
    all_to_all x2, waiting for transfers between devices, exchange(): return lax.all_to_all(value, axis, split_axis=0, concat_axis=0, tiled=True)  12.1 us
    pallas_call x1, Pallas kernels, attend_forward(): pl.pallas_call(functools.partial(forward_kernel, n=n, rows=rows), out_sha...  10.9 us
    pallas_call x2, Pallas kernels, expert_rows(): pl.pallas_call(functools.partial(expert_kernel, m=m), out_shape=[shaped((...  10.4 us
    all_to_all x2, starting transfers between devices, exchange(): return lax.all_to_all(value, axis, split_axis=0, concat_axis=0, tiled=True)  8.08 us
  transfers between devices with their start and end apart: 60, of which 25 were waited for; matrix products, arithmetic and copies ran while one was open for 12% of the time, Pallas kernels for 24%

profile of v1, /device:TPU:0, one launch (start us, length us, event | category | flops | bytes accessed | tf_op | source)
XLA Modules:
  0.0 294.8 jit_solution(16920279695120677127)
XLA Ops:
  10.7 4.0 %collective-permute-start.17 = (bf16[80,1024]{1,0:T(8,128)(2,1)}, bf16[80,1024]{1,0:T(8,128)(2,1)}, u32[]{:S(2)}, u32[]{:S(2)}) collective-permute-start(bf16[80,1024]{1,0:T(8,128)(2,1)} %get-tuple-element.185), channel_id=1, source_target_pairs={{0,24},{8,16},{16,8},{24,0},{1,25},{9,17},{17,9},{25,1},{2,26},{10... | collective-permute-start | bytes 491528 | tf_op jit(solution)/shard_map/ppermute | solution.py:24
  18.9 9.6 %collective-permute-done.2.refs_3_ = bf16[256,1024]{1,0:T(8,128)(2,1)} collective-permute-done((bf16[256,1024]{1,0:T(8,128)(2,1)S(1)}, bf16[256,1024]{1,0:T(8,128)(2,1)}, u32[]{:S(2)}, u32[]{:S(2)}) %collective-permute-start.2) | collective-permute-done | bytes 524320 | tf_op jit(solution)/shard_map/ppermute | solution.py:24
  30.9 10.9 %shard_map.170 = (bf16[1024,1024]{1,0:T(8,128)(2,1)}, f32[256,1]{1,0:T(8,128)S(1)}, bf16[1024,256]{1,0:T(8,128)(2,1)S(1)}, bf16[1024,256]{1,0:T(8,128)(2,1)S(1)}...) custom-call(s32[3]{0:T(128)S(1)} %pad_add_fusion.ids_ref, ...), custom_call_target="tpu_custom_call" | custom-call | flops 738197504 | bytes 2490368 | tf_op jit(solution)/shard_map/pallas_call | solution.py:140
  42.4 4.4 %collective-permute-done.3.refs_4_ = bf16[768,512]{1,0:T(8,128)(2,1)S(1)} collective-permute-done((bf16[768,512]{1,0:T(8,128)(2,1)S(1)}, bf16[768,512]{1,0:T(8,128)(2,1)S(1)}, u32[]{:S(2)}, u32[]{:S(2)}) %collective-permute-start.3) | collective-permute-done | bytes 786464 | tf_op jit(solution)/shard_map/ppermute | solution.py:24
  63.5 4.7 %collective-permute-done.18 = bf16[320,1024]{1,0:T(8,128)(2,1)S(1)} collective-permute-done((bf16[320,1024]{1,0:T(8,128)(2,1)S(1)}, bf16[320,1024]{1,0:T(8,128)(2,1)S(1)}, u32[]{:S(2)}, u32[]{:S(2)}) %collective-permute-start.18) | collective-permute-done | bytes 655392 | tf_op jit(solution)/shard_map/ppermute | solution.py:24
  70.6 4.5 %collective-permute-done.7 = bf16[80,1024]{1,0:T(8,128)(2,1)S(1)} collective-permute-done((bf16[80,1024]{1,0:T(8,128)(2,1)S(1)}, bf16[80,1024]{1,0:T(8,128)(2,1)S(1)}, u32[]{:S(2)}, u32[]{:S(2)}) %collective-permute-start.7) | collective-permute-done | bytes 163872 | tf_op jit(solution)/shard_map/ppermute | solution.py:24
  77.2 8.6 %collective-permute-done.12 = bf16[160,1024]{1,0:T(8,128)(2,1)S(1)} collective-permute-done((bf16[160,1024]{1,0:T(8,128)(2,1)S(1)}, bf16[160,1024]{1,0:T(8,128)(2,1)S(1)}, u32[]{:S(2)}, u32[]{:S(2)}) %collective-permute-start.12) | collective-permute-done | bytes 327712 | tf_op jit(solution)/shard_map/ppermute | solution.py:24
  85.9 5.5 %collective-permute-done.8 = bf16[160,1024]{1,0:T(8,128)(2,1)S(1)} collective-permute-done((bf16[160,1024]{1,0:T(8,128)(2,1)S(1)}, bf16[160,1024]{1,0:T(8,128)(2,1)S(1)}, u32[]{:S(2)}, u32[]{:S(2)}) %collective-permute-start.8) | collective-permute-done | bytes 327712 | tf_op jit(solution)/shard_map/ppermute | solution.py:24
  92.0 5.1 %shard_map.172 = (bf16[320,1024]{1,0:T(8,128)(2,1)S(1)}, bf16[320,1024]{1,0:T(8,128)(2,1)S(1)}, bf16[640,1024]{1,0:T(8,128)(2,1)S(1)}, bf16[640,1024]{1,0:T(8,128)(2,1)S(1)}) custom-call(bf16[640,1024]{1,0:T(8,128)(2,1)S(1)} %constant_dynamic-update-slice_fusion.refs_0_.refs_1_, bf16[640,1024]{1,0:T(8,128)(2,1)S(1)} %bitcast.66, ...), custom_call_target="tpu_custom_call" | custom-call | flops 1006632960 | bytes 2359296 | tf_op jit(solution)/shard_map/pallas_call | solution.py:254
  97.7 5.3 %shard_map.173 = (bf16[320,1024]{1,0:T(8,128)(2,1)S(1)}, bf16[320,1024]{1,0:T(8,128)(2,1)S(1)}, bf16[640,1024]{1,0:T(8,128)(2,1)S(1)}, bf16[640,1024]{1,0:T(8,128)(2,1)S(1)}) custom-call(bf16[640,1024]{1,0:T(8,128)(2,1)S(1)} %pad_maximum_fusion.1.refs_0_, bf16[640,1024]{1,0:T(8,128)(2,1)S(1)} %bitcast.64, bf16[1024,512]{1,0:T(8,128)(2,1)S(1)} %bitcast.69, ...), custom_call_target="tpu_custom_call" | custom-call | flops 1006632960 | bytes 2359296 | tf_op jit(solution)/shard_map/pallas_call | solution.py:254
  107.7 4.6 %shard_map.177 = (f32[512,1024]{1,0:T(8,128)S(1)}, bf16[512,1024]{1,0:T(8,128)(2,1)S(1)}) custom-call(bf16[640,1024]{1,0:T(8,128)(2,1)S(1)} %get-tuple-element.130.refs_0_, bf16[640,1024]{1,0:T(8,128)(2,1)S(1)} %get-tuple-element.131.refs_1_, bf16[640,1024]{1,0:T(8,128)(2,1)S(1)} %bitcast.65, bf16[640,1024]{1,0:T(8,128)(2,1)S(1)} %bitcast.67), custom_call_target="tpu_custom_call" | custom-call | flops 671088640 | bytes 2097152 | tf_op jit(solution)/shard_map/pallas_call | solution.py:400
  123.4 5.1 %shard_map.175 = (f32[1024,512]{1,0:T(8,128)S(1)}, bf16[1024,512]{1,0:T(8,128)(2,1)}) custom-call(bf16[640,1024]{1,0:T(8,128)(2,1)S(1)} %pad_maximum_fusion.1.refs_0_, bf16[640,1024]{1,0:T(8,128)(2,1)S(1)} %constant_dynamic-update-slice_fusion.refs_0_.refs_1_, bf16[640,1024]{1,0:T(8,128)(2,1)S(1)} %get-tuple-element.120.refs_2_, ...), custom_call_target="tpu_custom_call" | custom-call | flops 671088640 | bytes 2097152 | tf_op jit(solution)/shard_map/pallas_call | solution.py:355
  129.9 4.8 %shard_map.174 = (bf16[2,320,1024]{2,1,0:T(8,128)(2,1)S(1)}, bf16[2,320,1024]{2,1,0:T(8,128)(2,1)}) custom-call(bf16[640,1024]{1,0:T(8,128)(2,1)S(1)} %get-tuple-element.130.refs_0_, bf16[640,1024]{1,0:T(8,128)(2,1)S(1)} %get-tuple-element.131.refs_1_, bf16[512,1024]{1,0:T(8,128)(2,1)S(1)} %bitcast.63, ...), custom_call_target="tpu_custom_call" | custom-call | flops 671088640 | bytes 1835008 | tf_op jit(solution)/shard_map/pallas_call | solution.py:448
  135.8 4.1 %shard_map.176 = (f32[256,1024]{1,0:T(8,128)S(1)}, bf16[4,256,256]{2,1,0:T(8,128)(2,1)S(1)}, f32[4096,128]{1,0:T(8,128)S(1)}, bf16[4112,128]{1,0:T(8,128)(2,1)S(1)}) custom-call(s32[3]{0:T(128)S(1)} %pad_add_fusion.ids_ref, bf16[80,1024]{1,0:T(8,128)(2,1)S(1)} %get-tuple-element.124.refs_0_, bf16[80,1024]{1,0:T(8,128)(2,1)S(1)} %collective-permute-done.23.refs_1_, ...), custom_call_target="tpu_custom_call" | custom-call | flops 335544320 | bytes 2621440 | tf_op jit(solution)/shard_map/pallas_call | solution.py:321
  155.1 16.8 %shard_map.178 = (bf16[4,3,256,256]{3,2,1,0:T(8,128)(2,1)}, f32[4,768,128]{2,1,0:T(8,128)}, bf16[4,768,128]{2,1,0:T(8,128)(2,1)S(1)}) custom-call(s32[3]{0:T(128)S(1)} %pad_add_fusion.ids_ref, s32[1,1024]{1,0:T(1,128)S(1)} %bitcast.81, bf16[1024,1024]{1,0:T(8,128)(2,1)} %get-tuple-element.111.normed_ref, bf16[1024,256]{1,0:T(8,128)(2,1)S(1)} %copy-done.22, ...), custom_call_target="tpu_custom_call" | custom-call | flops 1241513984 | bytes 2686976 | tf_op jit(solution)/shard_map/pallas_call | solution.py:558
  185.9 10.6 %all-to-all-done.d_ref = bf16[4,3,256,256]{3,2,1,0:T(8,128)(2,1)S(1)} async-done(((bf16[4,3,256,256]{3,2,1,0:T(8,128)(2,1)}), bf16[4,3,256,256]{3,2,1,0:T(8,128)(2,1)S(1)}, u32[]{:S(2)}, u32[]{:S(2)}) %all-to-all-start) | async-done | bytes 1572896 | tf_op jit(solution)/shard_map/all_to_all | solution.py:28
  202.3 6.0 %collective-permute-done.39 = bf16[1040,128]{1,0:T(8,128)(2,1)S(1)} collective-permute-done((bf16[1040,128]{1,0:T(8,128)(2,1)}, bf16[1040,128]{1,0:T(8,128)(2,1)S(1)}, u32[]{:S(2)}, u32[]{:S(2)}) %collective-permute-start.39) | collective-permute-done | bytes 266272 | tf_op jit(solution)/shard_map/ppermute | solution.py:24
  215.1 4.5 %all-to-all-start.1 = ((bf16[4,1024,128]{2,1,0:T(8,128)(2,1)}), bf16[4,1024,128]{2,1,0:T(8,128)(2,1)}, u32[]{:S(2)}, u32[]{:S(2)}) async-start(bf16[4,1024,128]{2,1,0:T(8,128)(2,1)} %broadcast_in_dim.95), calls=%async_computation.1 | async-start | bytes 2097152 | tf_op jit(solution)/shard_map/all_to_all | solution.py:28
  220.7 12.9 %collective-permute-done.42 = bf16[1024,128]{1,0:T(8,128)(2,1)S(1)} collective-permute-done((bf16[1024,128]{1,0:T(8,128)(2,1)S(1)}, bf16[1024,128]{1,0:T(8,128)(2,1)S(1)}, u32[]{:S(2)}, u32[]{:S(2)}) %collective-permute-start.42) | collective-permute-done | bytes 262176 | tf_op jit(solution)/shard_map/ppermute | solution.py:24
  244.4 6.4 %collective-permute-done.47 = bf16[80,1024]{1,0:T(8,128)(2,1)S(1)} collective-permute-done((bf16[80,1024]{1,0:T(8,128)(2,1)S(1)}, bf16[80,1024]{1,0:T(8,128)(2,1)S(1)}, u32[]{:S(2)}, u32[]{:S(2)}) %collective-permute-start.47) | collective-permute-done | bytes 163872 | tf_op jit(solution)/shard_map/ppermute | solution.py:24
  251.5 6.2 %collective-permute-start.45 = (bf16[80,1024]{1,0:T(8,128)(2,1)}, bf16[80,1024]{1,0:T(8,128)(2,1)}, u32[]{:S(2)}, u32[]{:S(2)}) collective-permute-start(bf16[80,1024]{1,0:T(8,128)(2,1)} %get-tuple-element.184), channel_id=1, source_target_pairs={{0,8},{8,0},{16,24},{24,16},{1,9},{9,1},{17,25},{25,17},{2,10},{10... | collective-permute-start | bytes 491528 | tf_op jit(solution)/shard_map/ppermute | solution.py:24
  273.5 4.0 %shard_map.180 = f32[256,1024]{1,0:T(8,128)} custom-call(bf16[4,3,256,256]{3,2,1,0:T(8,128)(2,1)S(1)} %copy-done.6, bf16[1024,3072]{1,0:T(8,128)(2,1)S(1)} %bitcast.57, bf16[256,1024]{1,0:T(8,128)(2,1)S(1)} %bitcast.75, f32[256,1]{1,0:T(8,128)S(1)} %copy-done.28, f32[1,1024]{1,0:T(1,128)S(1)} %bitcast.78, f32[256,1024]{1,0:T(8,128)S(1)} %copy-done.16), custom_call_target="tpu_custom_call" | custom-call | flops 402653184 | bytes 2621440 | tf_op jit(solution)/shard_map/pallas_call | solution.py:764
  281.1 6.6 %shard_map.181 = (f32[1024,3072]{1,0:T(8,128)}, f32[1024,1024]{1,0:T(8,128)}, f32[1024,128]{1,0:T(8,128)S(1)}) custom-call(s32[3]{0:T(128)S(1)} %pad_add_fusion.ids_ref, bf16[4,1024,128]{2,1,0:T(8,128)(2,1)} %all-to-all-done.1.near_ref, bf16[3072,128]{1,0:T(8,128)(2,1)S(1)} %pad_maximum_fusion.4.refs_0_, bf16[3072,128]{1,0:T(8,128)(2,1)} %collective-permute-done.48.refs_1_, ...), custom_call_target="tpu_custom_call" | custom-call | flops 786432 | bytes 4194304 | tf_op jit(solution)/shard_map/pallas_call | solution.py:707
  287.8 6.2 %shard_map.182 = (f32[1024,3072]{1,0:T(8,128)}, f32[1024,1024]{1,0:T(8,128)}, f32[1024,128]{1,0:T(8,128)S(1)}) custom-call(s32[3]{0:T(128)S(1)} %pad_add_fusion.ids_ref, bf16[4,1024,128]{2,1,0:T(8,128)(2,1)} %collective-permute-done.50.near_ref, ...), custom_call_target="tpu_custom_call", output_to_operand_aliasing={{0}: (8, {}), {1}: (9, {}), {2}: (10, {})} | custom-call | flops 786432 | bytes 4194304 | tf_op jit(solution)/shard_map/pallas_call | solution.py:707
  (281 shorter events, 131.9 us)
Async XLA Ops:
  9.9 18.6 %collective-permute-start.2 = (bf16[256,1024]{1,0:T(8,128)(2,1)S(1)}, bf16[256,1024]{1,0:T(8,128)(2,1)}, u32[]{:S(2)}, u32[]{:S(2)}) collective-permute-start(bf16[256,1024]{1,0:T(8,128)(2,1)S(1)} %bitcast.72), channel_id=1, source_target_pairs={{0,6},{2,4},{4,2},{6,0},{1,7},{3,5},{5,3},{7,1},{8,14},{10,12},{12... | collective-permute-start | bytes 1572872 | tf_op jit(solution)/shard_map/ppermute | solution.py:24
  10.7 36.2 %collective-permute-start.17 = (bf16[80,1024]{1,0:T(8,128)(2,1)}, bf16[80,1024]{1,0:T(8,128)(2,1)}, u32[]{:S(2)}, u32[]{:S(2)}) collective-permute-start(bf16[80,1024]{1,0:T(8,128)(2,1)} %get-tuple-element.185), channel_id=1, source_target_pairs={{0,24},{8,16},{16,8},{24,0},{1,25},{9,17},{17,9},{25,1},{2,26},{10... | collective-permute-start | bytes 491528 | tf_op jit(solution)/shard_map/ppermute | solution.py:24
  14.7 32.1 %collective-permute-start.16 = (bf16[80,1024]{1,0:T(8,128)(2,1)}, bf16[80,1024]{1,0:T(8,128)(2,1)}, u32[]{:S(2)}, u32[]{:S(2)}) collective-permute-start(bf16[80,1024]{1,0:T(8,128)(2,1)} %get-tuple-element.186), channel_id=1, source_target_pairs={{0,16},{8,24},{16,0},{24,8},{1,17},{9,25},{17,1},{25,9},{2,18},{10... | collective-permute-start | bytes 491528 | tf_op jit(solution)/shard_map/ppermute | solution.py:24
  15.9 30.9 %collective-permute-start.15 = (bf16[80,1024]{1,0:T(8,128)(2,1)S(1)}, bf16[80,1024]{1,0:T(8,128)(2,1)S(1)}, u32[]{:S(2)}, u32[]{:S(2)}) collective-permute-start(bf16[80,1024]{1,0:T(8,128)(2,1)S(1)} %get-tuple-element.187), channel_id=1, source_target_pairs={{0,8},{8,0},{16,24},{24,16},{1,9},{9,1},{17,25},{25,17},{2,10},{10... | collective-permute-start | bytes 491528 | tf_op jit(solution)/shard_map/ppermute | solution.py:24
  56.2 29.7 %collective-permute-start.13 = (bf16[1280,512]{1,0:T(8,128)(2,1)S(1)}, bf16[1280,512]{1,0:T(8,128)(2,1)S(1)}, u32[]{:S(2)}, u32[]{:S(2)}) collective-permute-start(bf16[1280,512]{1,0:T(8,128)(2,1)S(1)} %pad_maximum_fusion.2), channel_id=1, source_target_pairs={{0,4},{2,6},{4,0},{6,2},{1,5},{3,7},{5,1},{7,3},{8,12},{10,14},{12... | collective-permute-start | bytes 3932168 | tf_op jit(solution)/shard_map/ppermute | solution.py:24
  68.4 23.3 %collective-permute-start.19 = (bf16[2,320,1024]{2,1,0:T(8,128)(2,1)S(1)}, bf16[2,320,1024]{2,1,0:T(8,128)(2,1)S(1)}, u32[]{:S(2)}, u32[]{:S(2)}) collective-permute-start(bf16[2,320,1024]{2,1,0:T(8,128)(2,1)S(1)} %get-tuple-element.174), channel_id=1, source_target_pairs={{0,1},{1,0},{2,3},{3,2},{4,5},{5,4},{6,7},{7,6},{8,9},{9,8},{10,11... | collective-permute-start | bytes 3932168 | tf_op jit(solution)/shard_map/ppermute | solution.py:24
  112.2 27.8 %collective-permute-start.28 = (bf16[512,1024]{1,0:T(8,128)(2,1)S(1)}, bf16[512,1024]{1,0:T(8,128)(2,1)S(1)}, u32[]{:S(2)}, u32[]{:S(2)}) collective-permute-start(bf16[512,1024]{1,0:T(8,128)(2,1)S(1)} %get-tuple-element.132), channel_id=1, source_target_pairs={{0,4},{2,6},{4,0},{6,2},{1,5},{3,7},{5,1},{7,3},{8,12},{10,14},{12... | collective-permute-start | bytes 3145736 | tf_op jit(solution)/shard_map/ppermute | solution.py:24
  116.1 18.6 %collective-permute-start.27 = (bf16[80,1024]{1,0:T(8,128)(2,1)S(1)}, bf16[80,1024]{1,0:T(8,128)(2,1)S(1)}, u32[]{:S(2)}, u32[]{:S(2)}) collective-permute-start(bf16[80,1024]{1,0:T(8,128)(2,1)S(1)} %get-tuple-element.201), channel_id=1, source_target_pairs={{0,24},{8,16},{16,8},{24,0},{1,25},{9,17},{17,9},{25,1},{2,26},{10... | collective-permute-start | bytes 491528 | tf_op jit(solution)/shard_map/ppermute | solution.py:24
  151.6 20.4 %collective-permute-start.33 = (bf16[1040,128]{1,0:T(8,128)(2,1)S(1)}, bf16[1040,128]{1,0:T(8,128)(2,1)S(1)}, u32[]{:S(2)}, u32[]{:S(2)}) collective-permute-start(bf16[1040,128]{1,0:T(8,128)(2,1)S(1)} %get-tuple-element.136), channel_id=1, source_target_pairs={{0,2},{2,0},{4,6},{6,4},{1,3},{3,1},{5,7},{7,5},{8,10},{10,8},{12,... | collective-permute-start | bytes 798728 | tf_op jit(solution)/shard_map/ppermute | solution.py:24
  153.0 18.9 %collective-permute-start.34 = (bf16[1040,128]{1,0:T(8,128)(2,1)S(1)}, bf16[1040,128]{1,0:T(8,128)(2,1)S(1)}, u32[]{:S(2)}, u32[]{:S(2)}) collective-permute-start(bf16[1040,128]{1,0:T(8,128)(2,1)S(1)} %get-tuple-element.137), channel_id=1, source_target_pairs={{0,4},{2,6},{4,0},{6,2},{1,5},{3,7},{5,1},{7,3},{8,12},{10,14},{12... | collective-permute-start | bytes 798728 | tf_op jit(solution)/shard_map/ppermute | solution.py:24
  155.1 41.4 %collective-permute-start.21 = (bf16[2,320,1024]{2,1,0:T(8,128)(2,1)}, bf16[2,320,1024]{2,1,0:T(8,128)(2,1)}, u32[]{:S(2)}, u32[]{:S(2)}) collective-permute-start(bf16[2,320,1024]{2,1,0:T(8,128)(2,1)} %get-tuple-element.110), channel_id=1, source_target_pairs={{0,1},{1,0},{2,3},{3,2},{4,5},{5,4},{6,7},{7,6},{8,9},{9,8},{10,11... | collective-permute-start | bytes 3932168 | tf_op jit(solution)/shard_map/ppermute | solution.py:24
  172.8 23.7 %all-to-all-start = ((bf16[4,3,256,256]{3,2,1,0:T(8,128)(2,1)}), bf16[4,3,256,256]{3,2,1,0:T(8,128)(2,1)S(1)}, u32[]{:S(2)}, u32[]{:S(2)}) async-start(bf16[4,3,256,256]{3,2,1,0:T(8,128)(2,1)} %get-tuple-element.142), calls=%async_computation | async-start | bytes 3145728 | tf_op jit(solution)/shard_map/all_to_all | solution.py:28
  181.5 20.9 %collective-permute-start.38 = (bf16[1040,128]{1,0:T(8,128)(2,1)}, bf16[1040,128]{1,0:T(8,128)(2,1)S(1)}, u32[]{:S(2)}, u32[]{:S(2)}) collective-permute-start(bf16[1040,128]{1,0:T(8,128)(2,1)} %get-tuple-element.147), channel_id=1, source_target_pairs={{0,24},{8,16},{16,8},{24,0},{1,25},{9,17},{17,9},{25,1},{2,26},{10... | collective-permute-start | bytes 798728 | tf_op jit(solution)/shard_map/ppermute | solution.py:24
  184.0 24.4 %collective-permute-start.39 = (bf16[1040,128]{1,0:T(8,128)(2,1)}, bf16[1040,128]{1,0:T(8,128)(2,1)S(1)}, u32[]{:S(2)}, u32[]{:S(2)}) collective-permute-start(bf16[1040,128]{1,0:T(8,128)(2,1)} %get-tuple-element.148), channel_id=1, source_target_pairs={{0,16},{8,24},{16,0},{24,8},{1,17},{9,25},{17,1},{25,9},{2,18},{10... | collective-permute-start | bytes 798728 | tf_op jit(solution)/shard_map/ppermute | solution.py:24
  184.1 24.2 %collective-permute-start.40 = (bf16[1040,128]{1,0:T(8,128)(2,1)}, bf16[1040,128]{1,0:T(8,128)(2,1)}, u32[]{:S(2)}, u32[]{:S(2)}) collective-permute-start(bf16[1040,128]{1,0:T(8,128)(2,1)} %get-tuple-element.149), channel_id=1, source_target_pairs={{0,8},{8,0},{16,24},{24,16},{1,9},{9,1},{17,25},{25,17},{2,10},{10... | collective-permute-start | bytes 798728 | tf_op jit(solution)/shard_map/ppermute | solution.py:24
  200.4 33.3 %collective-permute-start.36 = (bf16[320,1024]{1,0:T(8,128)(2,1)}, bf16[320,1024]{1,0:T(8,128)(2,1)}, u32[]{:S(2)}, u32[]{:S(2)}) collective-permute-start(bf16[320,1024]{1,0:T(8,128)(2,1)} %fusion.4), channel_id=1, source_target_pairs={{0,2},{2,0},{4,6},{6,4},{1,3},{3,1},{5,7},{7,5},{8,10},{10,8},{12,... | collective-permute-start | bytes 1966088 | tf_op jit(solution)/shard_map/ppermute | solution.py:24
  201.8 36.0 %collective-permute-start.44 = (bf16[1024,512]{1,0:T(8,128)(2,1)}, bf16[1024,512]{1,0:T(8,128)(2,1)}, u32[]{:S(2)}, u32[]{:S(2)}) collective-permute-start(bf16[1024,512]{1,0:T(8,128)(2,1)} %get-tuple-element.150), channel_id=1, source_target_pairs={{0,4},{2,6},{4,0},{6,2},{1,5},{3,7},{5,1},{7,3},{8,12},{10,14},{12... | collective-permute-start | bytes 3145736 | tf_op jit(solution)/shard_map/ppermute | solution.py:24
  212.2 21.3 %collective-permute-start.42 = (bf16[1024,128]{1,0:T(8,128)(2,1)S(1)}, bf16[1024,128]{1,0:T(8,128)(2,1)S(1)}, u32[]{:S(2)}, u32[]{:S(2)}) collective-permute-start(bf16[1024,128]{1,0:T(8,128)(2,1)S(1)} %add_convert_fusion), channel_id=1, source_target_pairs={{0,16},{8,24},{16,0},{24,8},{1,17},{9,25},{17,1},{25,9},{2,18},{10... | collective-permute-start | bytes 786440 | tf_op jit(solution)/shard_map/ppermute | solution.py:24
  212.2 21.3 %collective-permute-start.41 = (bf16[1024,128]{1,0:T(8,128)(2,1)S(1)}, bf16[1024,128]{1,0:T(8,128)(2,1)S(1)}, u32[]{:S(2)}, u32[]{:S(2)}) collective-permute-start(bf16[1024,128]{1,0:T(8,128)(2,1)S(1)} %add_convert_fusion), channel_id=1, source_target_pairs={{0,8},{8,0},{16,24},{24,16},{1,9},{9,1},{17,25},{25,17},{2,10},{10... | collective-permute-start | bytes 786440 | tf_op jit(solution)/shard_map/ppermute | solution.py:24
  215.1 22.7 %all-to-all-start.1 = ((bf16[4,1024,128]{2,1,0:T(8,128)(2,1)}), bf16[4,1024,128]{2,1,0:T(8,128)(2,1)}, u32[]{:S(2)}, u32[]{:S(2)}) async-start(bf16[4,1024,128]{2,1,0:T(8,128)(2,1)} %broadcast_in_dim.95), calls=%async_computation.1 | async-start | bytes 2097152 | tf_op jit(solution)/shard_map/all_to_all | solution.py:28
  237.8 35.1 %collective-permute-start.50 = (bf16[4,1024,128]{2,1,0:T(8,128)(2,1)}, bf16[4,1024,128]{2,1,0:T(8,128)(2,1)}, u32[]{:S(2)}, u32[]{:S(2)}) collective-permute-start(bf16[4,1024,128]{2,1,0:T(8,128)(2,1)} %all-to-all-done.1.near_ref), channel_id=1, source_target_pairs={{0,1},{1,0},{2,3},{3,2},{4,5},{5,4},{6,7},{7,6},{8,9},{9,8},{10,11... | collective-permute-start | bytes 3145736 | tf_op jit(solution)/shard_map/ppermute | solution.py:24
  237.8 28.0 %collective-permute-start.49 = (bf16[3072,128]{1,0:T(8,128)(2,1)S(1)}, bf16[3072,128]{1,0:T(8,128)(2,1)}, u32[]{:S(2)}, u32[]{:S(2)}) collective-permute-start(bf16[3072,128]{1,0:T(8,128)(2,1)S(1)} %pad_maximum_fusion.4.refs_0_), channel_id=1, source_target_pairs={{0,4},{2,6},{4,0},{6,2},{1,5},{3,7},{5,1},{7,3},{8,12},{10,14},{12... | collective-permute-start | bytes 2359304 | tf_op jit(solution)/shard_map/ppermute | solution.py:24
  238.4 29.1 %collective-permute-start.48 = (bf16[3072,128]{1,0:T(8,128)(2,1)S(1)}, bf16[3072,128]{1,0:T(8,128)(2,1)}, u32[]{:S(2)}, u32[]{:S(2)}) collective-permute-start(bf16[3072,128]{1,0:T(8,128)(2,1)S(1)} %pad_maximum_fusion.4.refs_0_), channel_id=1, source_target_pairs={{0,2},{2,0},{4,6},{6,4},{1,3},{3,1},{5,7},{7,5},{8,10},{10,8},{12,... | collective-permute-start | bytes 2359304 | tf_op jit(solution)/shard_map/ppermute | solution.py:24
  259.5 28.2 %collective-permute-start.51 = (bf16[3072,128]{1,0:T(8,128)(2,1)S(1)}, bf16[3072,128]{1,0:T(8,128)(2,1)S(1)}, u32[]{:S(2)}, u32[]{:S(2)}) collective-permute-start(bf16[3072,128]{1,0:T(8,128)(2,1)S(1)} %pad_maximum_fusion.4.refs_0_), channel_id=1, source_target_pairs={{0,1},{1,0},{2,3},{3,2},{4,5},{5,4},{6,7},{7,6},{8,9},{9,8},{10,11... | collective-permute-start | bytes 2359304 | tf_op jit(solution)/shard_map/ppermute | solution.py:24
  (87 other events, 833.7 us)

commit v2 on v0

--- a/solution.py
+++ b/solution.py
@@ -962,13 +962,16 @@
     near_lines = spread_to(piece, "ctx")
     line = jnp.concatenate([arrived[k] for k in range(1, owners)], axis=0)
     line = after(line, in_others, made_own, near_lines)
+    returned = send_rows(after(made_own, line))
     if n == 4:
         half = line.shape[0] // 2
         one, two = swap(line, "ctx", 1), swap(line, "ctx", 2)
         sent = (one[:half], two[half:])
         last = [swap(sent[0], "ctx", 2), swap(sent[1], "ctx", 1)]
         far_lines = [[line], [one], [two], last]
-        in_others, out_others, d_pieces = after((in_others, out_others, d_pieces), sent)
+        in_others, out_others, d_pieces, returned = after(
+            (in_others, out_others, d_pieces, returned), sent
+        )
     else:
         far_lines = [[line]] + [[swap(line, "ctx", r)] for r in range(1, n)]
     grad_inputs = back_to_tokens(
@@ -981,7 +984,7 @@
     )
     grad_expert_out = add_others(grads_out[0], out_others)
     grad_expert_in = add_others(grads_in[0], in_others)
-    returned = jnp.concatenate(send_rows(after(made_own, line)), axis=0)
+    returned = jnp.concatenate(returned, axis=0)
     block_out = (
         hidden + matmul(places.transpose(1, 0, 2).reshape(rows, slots), returned)
     ).astype(BF16)

time: 295 us -> 291 us (0.986)
  starting transfers between devices: 75.5 us -> 70.1 us
    ppermute x58, starting transfers between devices: 67.4 us -> 62 us  [swap(): return lax.ppermute(value, axis, [(i, i ^ bits) for i in range(size)])]
  transfers between devices with their start and end apart: 60 -> 60, of which waited for: 28 -> 27; matrix products, arithmetic and copies ran while one was open for 12% -> 12% of each run, Pallas kernels for 24% -> 24%
where the time goes in v2:
time: 291 us; the launch traced here: 290 us
  waiting for transfers between devices  98.3 us (34%)
  Pallas kernels  75.9 us (26%)
  starting transfers between devices  70.1 us (24%)
  local copies, waits for them, and re-layouts  21.7 us (7%)
  other arithmetic  19.9 us (7%)
  matrix products  2.94 us (1%)
    ppermute x58, waiting for transfers between devices, swap(): return lax.ppermute(value, axis, [(i, i ^ bits) for i in range(size)])  86.1 us
    ppermute x58, starting transfers between devices, swap(): return lax.ppermute(value, axis, [(i, i ^ bits) for i in range(size)])  62 us
    pallas_call x1, Pallas kernels, attend_backward(): pl.pallas_call(functools.partial(backward_kernel, n=n, rows=rows, owners=...  16.8 us
    pallas_call x2, Pallas kernels, dense_out(): pl.pallas_call(functools.partial(dense_out_kernel, counts=counts, s=s, n=...  12.8 us
    all_to_all x2, waiting for transfers between devices, exchange(): return lax.all_to_all(value, axis, split_axis=0, concat_axis=0, tiled=True)  12.2 us
    pallas_call x1, Pallas kernels, attend_forward(): pl.pallas_call(functools.partial(forward_kernel, n=n, rows=rows), out_sha...  10.6 us
    pallas_call x2, Pallas kernels, expert_rows(): pl.pallas_call(functools.partial(expert_kernel, m=m), out_shape=[shaped((...  10.4 us
    all_to_all x2, starting transfers between devices, exchange(): return lax.all_to_all(value, axis, split_axis=0, concat_axis=0, tiled=True)  8.07 us
  transfers between devices with their start and end apart: 60, of which 27 were waited for; matrix products, arithmetic and copies ran while one was open for 12% of the time, Pallas kernels for 24%

profile of v2, /device:TPU:0, one launch (start us, length us, event | category | flops | bytes accessed | tf_op | source)
XLA Modules:
  0.0 290.4 jit_solution(2673989786027662808)
XLA Ops:
  10.7 4.0 %collective-permute-start.17 = (bf16[80,1024]{1,0:T(8,128)(2,1)}, bf16[80,1024]{1,0:T(8,128)(2,1)}, u32[]{:S(2)}, u32[]{:S(2)}) collective-permute-start(bf16[80,1024]{1,0:T(8,128)(2,1)} %get-tuple-element.188), channel_id=1, source_target_pairs={{0,24},{8,16},{16,8},{24,0},{1,25},{9,17},{17,9},{25,1},{2,26},{10... | collective-permute-start | bytes 491528 | tf_op jit(solution)/shard_map/ppermute | solution.py:24
  18.9 9.5 %collective-permute-done.2.refs_3_ = bf16[256,1024]{1,0:T(8,128)(2,1)S(1)} collective-permute-done((bf16[256,1024]{1,0:T(8,128)(2,1)S(1)}, bf16[256,1024]{1,0:T(8,128)(2,1)S(1)}, u32[]{:S(2)}, u32[]{:S(2)}) %collective-permute-start.2) | collective-permute-done | bytes 524320 | tf_op jit(solution)/shard_map/ppermute | solution.py:24
  34.3 10.6 %shard_map.170 = (bf16[1024,1024]{1,0:T(8,128)(2,1)}, f32[256,1]{1,0:T(8,128)S(1)}, bf16[1024,256]{1,0:T(8,128)(2,1)S(1)}, bf16[1024,256]{1,0:T(8,128)(2,1)S(1)}...) custom-call(s32[3]{0:T(128)S(1)} %pad_add_fusion.ids_ref, ...), custom_call_target="tpu_custom_call" | custom-call | flops 738197504 | bytes 2490368 | tf_op jit(solution)/shard_map/pallas_call | solution.py:140
  64.4 4.4 %collective-permute-done.18 = bf16[320,1024]{1,0:T(8,128)(2,1)S(1)} collective-permute-done((bf16[320,1024]{1,0:T(8,128)(2,1)S(1)}, bf16[320,1024]{1,0:T(8,128)(2,1)S(1)}, u32[]{:S(2)}, u32[]{:S(2)}) %collective-permute-start.18) | collective-permute-done | bytes 655392 | tf_op jit(solution)/shard_map/ppermute | solution.py:24
  71.6 4.1 %collective-permute-done.7 = bf16[80,1024]{1,0:T(8,128)(2,1)S(1)} collective-permute-done((bf16[80,1024]{1,0:T(8,128)(2,1)S(1)}, bf16[80,1024]{1,0:T(8,128)(2,1)S(1)}, u32[]{:S(2)}, u32[]{:S(2)}) %collective-permute-start.7) | collective-permute-done | bytes 163872 | tf_op jit(solution)/shard_map/ppermute | solution.py:24
  77.8 8.6 %collective-permute-done.12 = bf16[160,1024]{1,0:T(8,128)(2,1)S(1)} collective-permute-done((bf16[160,1024]{1,0:T(8,128)(2,1)S(1)}, bf16[160,1024]{1,0:T(8,128)(2,1)S(1)}, u32[]{:S(2)}, u32[]{:S(2)}) %collective-permute-start.12) | collective-permute-done | bytes 327712 | tf_op jit(solution)/shard_map/ppermute | solution.py:24
  86.6 5.5 %collective-permute-done.8 = bf16[160,1024]{1,0:T(8,128)(2,1)S(1)} collective-permute-done((bf16[160,1024]{1,0:T(8,128)(2,1)S(1)}, bf16[160,1024]{1,0:T(8,128)(2,1)S(1)}, u32[]{:S(2)}, u32[]{:S(2)}) %collective-permute-start.8) | collective-permute-done | bytes 327712 | tf_op jit(solution)/shard_map/ppermute | solution.py:24
  92.6 5.1 %shard_map.172 = (bf16[320,1024]{1,0:T(8,128)(2,1)S(1)}, bf16[320,1024]{1,0:T(8,128)(2,1)S(1)}, bf16[640,1024]{1,0:T(8,128)(2,1)S(1)}, bf16[640,1024]{1,0:T(8,128)(2,1)S(1)}) custom-call(bf16[640,1024]{1,0:T(8,128)(2,1)S(1)} %constant_dynamic-update-slice_fusion.refs_0_.refs_1_, bf16[640,1024]{1,0:T(8,128)(2,1)S(1)} %bitcast.66, ...), custom_call_target="tpu_custom_call" | custom-call | flops 1006632960 | bytes 2359296 | tf_op jit(solution)/shard_map/pallas_call | solution.py:254
  98.4 5.3 %shard_map.173 = (bf16[320,1024]{1,0:T(8,128)(2,1)S(1)}, bf16[320,1024]{1,0:T(8,128)(2,1)S(1)}, bf16[640,1024]{1,0:T(8,128)(2,1)S(1)}, bf16[640,1024]{1,0:T(8,128)(2,1)S(1)}) custom-call(bf16[640,1024]{1,0:T(8,128)(2,1)S(1)} %pad_maximum_fusion.1.refs_0_, bf16[640,1024]{1,0:T(8,128)(2,1)S(1)} %bitcast.64, bf16[1024,512]{1,0:T(8,128)(2,1)S(1)} %bitcast.69, ...), custom_call_target="tpu_custom_call" | custom-call | flops 1006632960 | bytes 2359296 | tf_op jit(solution)/shard_map/pallas_call | solution.py:254
  107.7 4.6 %shard_map.177 = (f32[512,1024]{1,0:T(8,128)S(1)}, bf16[512,1024]{1,0:T(8,128)(2,1)S(1)}) custom-call(bf16[640,1024]{1,0:T(8,128)(2,1)S(1)} %get-tuple-element.127.refs_0_, bf16[640,1024]{1,0:T(8,128)(2,1)S(1)} %get-tuple-element.128.refs_1_, bf16[640,1024]{1,0:T(8,128)(2,1)S(1)} %bitcast.65, bf16[640,1024]{1,0:T(8,128)(2,1)S(1)} %bitcast.67), custom_call_target="tpu_custom_call" | custom-call | flops 671088640 | bytes 2097152 | tf_op jit(solution)/shard_map/pallas_call | solution.py:400
  122.9 5.1 %shard_map.174 = (f32[1024,512]{1,0:T(8,128)S(1)}, bf16[1024,512]{1,0:T(8,128)(2,1)}) custom-call(bf16[640,1024]{1,0:T(8,128)(2,1)S(1)} %pad_maximum_fusion.1.refs_0_, bf16[640,1024]{1,0:T(8,128)(2,1)S(1)} %constant_dynamic-update-slice_fusion.refs_0_.refs_1_, bf16[640,1024]{1,0:T(8,128)(2,1)S(1)} %get-tuple-element.105.refs_2_, ...), custom_call_target="tpu_custom_call" | custom-call | flops 671088640 | bytes 2097152 | tf_op jit(solution)/shard_map/pallas_call | solution.py:355
  129.4 4.9 %shard_map.175 = (bf16[2,320,1024]{2,1,0:T(8,128)(2,1)S(1)}, bf16[2,320,1024]{2,1,0:T(8,128)(2,1)}) custom-call(bf16[640,1024]{1,0:T(8,128)(2,1)S(1)} %get-tuple-element.127.refs_0_, bf16[640,1024]{1,0:T(8,128)(2,1)S(1)} %get-tuple-element.128.refs_1_, bf16[512,1024]{1,0:T(8,128)(2,1)S(1)} %bitcast.63, ...), custom_call_target="tpu_custom_call" | custom-call | flops 671088640 | bytes 1835008 | tf_op jit(solution)/shard_map/pallas_call | solution.py:448
  135.3 4.2 %shard_map.176 = (f32[256,1024]{1,0:T(8,128)S(1)}, bf16[4,256,256]{2,1,0:T(8,128)(2,1)S(1)}, f32[4096,128]{1,0:T(8,128)S(1)}, bf16[4112,128]{1,0:T(8,128)(2,1)S(1)}) custom-call(s32[3]{0:T(128)S(1)} %pad_add_fusion.ids_ref, bf16[80,1024]{1,0:T(8,128)(2,1)S(1)} %get-tuple-element.121.refs_0_, bf16[80,1024]{1,0:T(8,128)(2,1)S(1)} %collective-permute-done.22.refs_1_, ...), custom_call_target="tpu_custom_call" | custom-call | flops 335544320 | bytes 2621440 | tf_op jit(solution)/shard_map/pallas_call | solution.py:321
  143.2 3.8 %collective-permute-done.30 = bf16[256,256]{1,0:T(8,128)(2,1)S(1)} collective-permute-done((bf16[256,256]{1,0:T(8,128)(2,1)S(1)}, bf16[256,256]{1,0:T(8,128)(2,1)S(1)}, u32[]{:S(2)}, u32[]{:S(2)}) %collective-permute-start.30) | collective-permute-done | bytes 131104 | tf_op jit(solution)/shard_map/ppermute | solution.py:24
  154.8 16.8 %shard_map.178 = (bf16[4,3,256,256]{3,2,1,0:T(8,128)(2,1)}, f32[4,768,128]{2,1,0:T(8,128)}, bf16[4,768,128]{2,1,0:T(8,128)(2,1)S(1)}) custom-call(s32[3]{0:T(128)S(1)} %pad_add_fusion.ids_ref, s32[1,1024]{1,0:T(1,128)S(1)} %bitcast.81, bf16[1024,1024]{1,0:T(8,128)(2,1)} %get-tuple-element.109.normed_ref, bf16[1024,256]{1,0:T(8,128)(2,1)S(1)} %copy-done.24, ...), custom_call_target="tpu_custom_call" | custom-call | flops 1241513984 | bytes 2686976 | tf_op jit(solution)/shard_map/pallas_call | solution.py:558
  172.4 3.6 %all-to-all-start = ((bf16[4,3,256,256]{3,2,1,0:T(8,128)(2,1)}), bf16[4,3,256,256]{3,2,1,0:T(8,128)(2,1)S(1)}, u32[]{:S(2)}, u32[]{:S(2)}) async-start(bf16[4,3,256,256]{3,2,1,0:T(8,128)(2,1)} %get-tuple-element.139), calls=%async_computation | async-start | bytes 3145728 | tf_op jit(solution)/shard_map/all_to_all | solution.py:28
  185.5 10.6 %all-to-all-done.d_ref = bf16[4,3,256,256]{3,2,1,0:T(8,128)(2,1)S(1)} async-done(((bf16[4,3,256,256]{3,2,1,0:T(8,128)(2,1)}), bf16[4,3,256,256]{3,2,1,0:T(8,128)(2,1)S(1)}, u32[]{:S(2)}, u32[]{:S(2)}) %all-to-all-start) | async-done | bytes 1572896 | tf_op jit(solution)/shard_map/all_to_all | solution.py:28
  202.0 6.0 %collective-permute-done.40 = bf16[1040,128]{1,0:T(8,128)(2,1)S(1)} collective-permute-done((bf16[1040,128]{1,0:T(8,128)(2,1)}, bf16[1040,128]{1,0:T(8,128)(2,1)S(1)}, u32[]{:S(2)}, u32[]{:S(2)}) %collective-permute-start.40) | collective-permute-done | bytes 266272 | tf_op jit(solution)/shard_map/ppermute | solution.py:24
  214.7 4.5 %all-to-all-start.1 = ((bf16[4,1024,128]{2,1,0:T(8,128)(2,1)}), bf16[4,1024,128]{2,1,0:T(8,128)(2,1)}, u32[]{:S(2)}, u32[]{:S(2)}) async-start(bf16[4,1024,128]{2,1,0:T(8,128)(2,1)} %broadcast_in_dim.95), calls=%async_computation.1 | async-start | bytes 2097152 | tf_op jit(solution)/shard_map/all_to_all | solution.py:28
  220.3 12.9 %collective-permute-done.43 = bf16[1024,128]{1,0:T(8,128)(2,1)S(1)} collective-permute-done((bf16[1024,128]{1,0:T(8,128)(2,1)S(1)}, bf16[1024,128]{1,0:T(8,128)(2,1)S(1)}, u32[]{:S(2)}, u32[]{:S(2)}) %collective-permute-start.43) | collective-permute-done | bytes 262176 | tf_op jit(solution)/shard_map/ppermute | solution.py:24
  244.2 11.3 %collective-permute-done.49.refs_2_ = bf16[3072,128]{1,0:T(8,128)(2,1)} collective-permute-done((bf16[3072,128]{1,0:T(8,128)(2,1)S(1)}, bf16[3072,128]{1,0:T(8,128)(2,1)}, u32[]{:S(2)}, u32[]{:S(2)}) %collective-permute-start.49) | collective-permute-done | bytes 786464 | tf_op jit(solution)/shard_map/ppermute | solution.py:24
  269.2 4.0 %shard_map.180 = f32[256,1024]{1,0:T(8,128)} custom-call(bf16[4,3,256,256]{3,2,1,0:T(8,128)(2,1)S(1)} %copy-done.6, bf16[1024,3072]{1,0:T(8,128)(2,1)S(1)} %bitcast.57, bf16[256,1024]{1,0:T(8,128)(2,1)S(1)} %bitcast.75, f32[256,1]{1,0:T(8,128)S(1)} %copy-done.36, f32[1,1024]{1,0:T(1,128)S(1)} %bitcast.78, f32[256,1024]{1,0:T(8,128)S(1)} %copy-done.17), custom_call_target="tpu_custom_call" | custom-call | flops 402653184 | bytes 2621440 | tf_op jit(solution)/shard_map/pallas_call | solution.py:764
  276.7 6.6 %shard_map.181 = (f32[1024,3072]{1,0:T(8,128)}, f32[1024,1024]{1,0:T(8,128)}, f32[1024,128]{1,0:T(8,128)S(1)}) custom-call(s32[3]{0:T(128)S(1)} %pad_add_fusion.ids_ref, bf16[4,1024,128]{2,1,0:T(8,128)(2,1)} %all-to-all-done.1.near_ref, bf16[3072,128]{1,0:T(8,128)(2,1)S(1)} %pad_maximum_fusion.4.refs_0_, bf16[3072,128]{1,0:T(8,128)(2,1)} %collective-permute-done.48.refs_1_, ...), custom_call_target="tpu_custom_call" | custom-call | flops 786432 | bytes 4194304 | tf_op jit(solution)/shard_map/pallas_call | solution.py:707
  283.4 6.2 %shard_map.182 = (f32[1024,3072]{1,0:T(8,128)}, f32[1024,1024]{1,0:T(8,128)}, f32[1024,128]{1,0:T(8,128)S(1)}) custom-call(s32[3]{0:T(128)S(1)} %pad_add_fusion.ids_ref, bf16[4,1024,128]{2,1,0:T(8,128)(2,1)} %collective-permute-done.50.near_ref, ...), custom_call_target="tpu_custom_call", output_to_operand_aliasing={{0}: (8, {}), {1}: (9, {}), {2}: (10, {})} | custom-call | flops 786432 | bytes 4194304 | tf_op jit(solution)/shard_map/pallas_call | solution.py:707
  (294 shorter events, 126.8 us)
Async XLA Ops:
  9.7 18.7 %collective-permute-start.2 = (bf16[256,1024]{1,0:T(8,128)(2,1)S(1)}, bf16[256,1024]{1,0:T(8,128)(2,1)S(1)}, u32[]{:S(2)}, u32[]{:S(2)}) collective-permute-start(bf16[256,1024]{1,0:T(8,128)(2,1)S(1)} %bitcast.72), channel_id=1, source_target_pairs={{0,6},{2,4},{4,2},{6,0},{1,7},{3,5},{5,3},{7,1},{8,14},{10,12},{12... | collective-permute-start | bytes 1572872 | tf_op jit(solution)/shard_map/ppermute | solution.py:24
  10.7 22.2 %collective-permute-start.17 = (bf16[80,1024]{1,0:T(8,128)(2,1)}, bf16[80,1024]{1,0:T(8,128)(2,1)}, u32[]{:S(2)}, u32[]{:S(2)}) collective-permute-start(bf16[80,1024]{1,0:T(8,128)(2,1)} %get-tuple-element.188), channel_id=1, source_target_pairs={{0,24},{8,16},{16,8},{24,0},{1,25},{9,17},{17,9},{25,1},{2,26},{10... | collective-permute-start | bytes 491528 | tf_op jit(solution)/shard_map/ppermute | solution.py:24
  14.7 18.3 %collective-permute-start.16 = (bf16[80,1024]{1,0:T(8,128)(2,1)}, bf16[80,1024]{1,0:T(8,128)(2,1)}, u32[]{:S(2)}, u32[]{:S(2)}) collective-permute-start(bf16[80,1024]{1,0:T(8,128)(2,1)} %get-tuple-element.189), channel_id=1, source_target_pairs={{0,16},{8,24},{16,0},{24,8},{1,17},{9,25},{17,1},{25,9},{2,18},{10... | collective-permute-start | bytes 491528 | tf_op jit(solution)/shard_map/ppermute | solution.py:24
  29.1 18.7 %collective-permute-start.3 = (bf16[768,512]{1,0:T(8,128)(2,1)}, bf16[768,512]{1,0:T(8,128)(2,1)S(1)}, u32[]{:S(2)}, u32[]{:S(2)}) collective-permute-start(bf16[768,512]{1,0:T(8,128)(2,1)} %slice_bitcast_fusion.1), channel_id=1, source_target_pairs={{0,4},{2,6},{4,0},{6,2},{1,5},{3,7},{5,1},{7,3},{8,12},{10,14},{12... | collective-permute-start | bytes 2359304 | tf_op jit(solution)/shard_map/ppermute | solution.py:24
  58.0 28.5 %collective-permute-start.13 = (bf16[1280,512]{1,0:T(8,128)(2,1)S(1)}, bf16[1280,512]{1,0:T(8,128)(2,1)S(1)}, u32[]{:S(2)}, u32[]{:S(2)}) collective-permute-start(bf16[1280,512]{1,0:T(8,128)(2,1)S(1)} %pad_maximum_fusion.2), channel_id=1, source_target_pairs={{0,4},{2,6},{4,0},{6,2},{1,5},{3,7},{5,1},{7,3},{8,12},{10,14},{12... | collective-permute-start | bytes 3932168 | tf_op jit(solution)/shard_map/ppermute | solution.py:24
  69.0 23.3 %collective-permute-start.19 = (bf16[2,320,1024]{2,1,0:T(8,128)(2,1)S(1)}, bf16[2,320,1024]{2,1,0:T(8,128)(2,1)S(1)}, u32[]{:S(2)}, u32[]{:S(2)}) collective-permute-start(bf16[2,320,1024]{2,1,0:T(8,128)(2,1)S(1)} %get-tuple-element.176), channel_id=1, source_target_pairs={{0,1},{1,0},{2,3},{3,2},{4,5},{5,4},{6,7},{7,6},{8,9},{9,8},{10,11... | collective-permute-start | bytes 3932168 | tf_op jit(solution)/shard_map/ppermute | solution.py:24
  112.2 27.3 %collective-permute-start.27 = (bf16[512,1024]{1,0:T(8,128)(2,1)S(1)}, bf16[512,1024]{1,0:T(8,128)(2,1)S(1)}, u32[]{:S(2)}, u32[]{:S(2)}) collective-permute-start(bf16[512,1024]{1,0:T(8,128)(2,1)S(1)} %get-tuple-element.129), channel_id=1, source_target_pairs={{0,4},{2,6},{4,0},{6,2},{1,5},{3,7},{5,1},{7,3},{8,12},{10,14},{12... | collective-permute-start | bytes 3145736 | tf_op jit(solution)/shard_map/ppermute | solution.py:24
  114.7 19.5 %collective-permute-start.26 = (bf16[80,1024]{1,0:T(8,128)(2,1)S(1)}, bf16[80,1024]{1,0:T(8,128)(2,1)S(1)}, u32[]{:S(2)}, u32[]{:S(2)}) collective-permute-start(bf16[80,1024]{1,0:T(8,128)(2,1)S(1)} %get-tuple-element.203), channel_id=1, source_target_pairs={{0,24},{8,16},{16,8},{24,0},{1,25},{9,17},{17,9},{25,1},{2,26},{10... | collective-permute-start | bytes 491528 | tf_op jit(solution)/shard_map/ppermute | solution.py:24
  151.2 20.4 %collective-permute-start.32 = (bf16[1040,128]{1,0:T(8,128)(2,1)S(1)}, bf16[1040,128]{1,0:T(8,128)(2,1)S(1)}, u32[]{:S(2)}, u32[]{:S(2)}) collective-permute-start(bf16[1040,128]{1,0:T(8,128)(2,1)S(1)} %get-tuple-element.133), channel_id=1, source_target_pairs={{0,2},{2,0},{4,6},{6,4},{1,3},{3,1},{5,7},{7,5},{8,10},{10,8},{12,... | collective-permute-start | bytes 798728 | tf_op jit(solution)/shard_map/ppermute | solution.py:24
  152.7 18.9 %collective-permute-start.33 = (bf16[1040,128]{1,0:T(8,128)(2,1)S(1)}, bf16[1040,128]{1,0:T(8,128)(2,1)S(1)}, u32[]{:S(2)}, u32[]{:S(2)}) collective-permute-start(bf16[1040,128]{1,0:T(8,128)(2,1)S(1)} %get-tuple-element.134), channel_id=1, source_target_pairs={{0,4},{2,6},{4,0},{6,2},{1,5},{3,7},{5,1},{7,3},{8,12},{10,14},{12... | collective-permute-start | bytes 798728 | tf_op jit(solution)/shard_map/ppermute | solution.py:24
  154.7 30.7 %collective-permute-start.36 = (bf16[2,320,1024]{2,1,0:T(8,128)(2,1)}, bf16[2,320,1024]{2,1,0:T(8,128)(2,1)}, u32[]{:S(2)}, u32[]{:S(2)}) collective-permute-start(bf16[2,320,1024]{2,1,0:T(8,128)(2,1)} %get-tuple-element.141), channel_id=1, source_target_pairs={{0,1},{1,0},{2,3},{3,2},{4,5},{5,4},{6,7},{7,6},{8,9},{9,8},{10,11... | collective-permute-start | bytes 3932168 | tf_op jit(solution)/shard_map/ppermute | solution.py:24
  172.4 23.7 %all-to-all-start = ((bf16[4,3,256,256]{3,2,1,0:T(8,128)(2,1)}), bf16[4,3,256,256]{3,2,1,0:T(8,128)(2,1)S(1)}, u32[]{:S(2)}, u32[]{:S(2)}) async-start(bf16[4,3,256,256]{3,2,1,0:T(8,128)(2,1)} %get-tuple-element.139), calls=%async_computation | async-start | bytes 3145728 | tf_op jit(solution)/shard_map/all_to_all | solution.py:28
  181.1 20.9 %collective-permute-start.39 = (bf16[1040,128]{1,0:T(8,128)(2,1)}, bf16[1040,128]{1,0:T(8,128)(2,1)S(1)}, u32[]{:S(2)}, u32[]{:S(2)}) collective-permute-start(bf16[1040,128]{1,0:T(8,128)(2,1)} %get-tuple-element.146), channel_id=1, source_target_pairs={{0,24},{8,16},{16,8},{24,0},{1,25},{9,17},{17,9},{25,1},{2,26},{10... | collective-permute-start | bytes 798728 | tf_op jit(solution)/shard_map/ppermute | solution.py:24
  183.6 24.4 %collective-permute-start.40 = (bf16[1040,128]{1,0:T(8,128)(2,1)}, bf16[1040,128]{1,0:T(8,128)(2,1)S(1)}, u32[]{:S(2)}, u32[]{:S(2)}) collective-permute-start(bf16[1040,128]{1,0:T(8,128)(2,1)} %get-tuple-element.147), channel_id=1, source_target_pairs={{0,16},{8,24},{16,0},{24,8},{1,17},{9,25},{17,1},{25,9},{2,18},{10... | collective-permute-start | bytes 798728 | tf_op jit(solution)/shard_map/ppermute | solution.py:24
  183.7 24.2 %collective-permute-start.41 = (bf16[1040,128]{1,0:T(8,128)(2,1)}, bf16[1040,128]{1,0:T(8,128)(2,1)}, u32[]{:S(2)}, u32[]{:S(2)}) collective-permute-start(bf16[1040,128]{1,0:T(8,128)(2,1)} %get-tuple-element.148), channel_id=1, source_target_pairs={{0,8},{8,0},{16,24},{24,16},{1,9},{9,1},{17,25},{25,17},{2,10},{10... | collective-permute-start | bytes 798728 | tf_op jit(solution)/shard_map/ppermute | solution.py:24
  200.0 33.3 %collective-permute-start.37 = (bf16[320,1024]{1,0:T(8,128)(2,1)}, bf16[320,1024]{1,0:T(8,128)(2,1)}, u32[]{:S(2)}, u32[]{:S(2)}) collective-permute-start(bf16[320,1024]{1,0:T(8,128)(2,1)} %fusion.4), channel_id=1, source_target_pairs={{0,2},{2,0},{4,6},{6,4},{1,3},{3,1},{5,7},{7,5},{8,10},{10,8},{12,... | collective-permute-start | bytes 1966088 | tf_op jit(solution)/shard_map/ppermute | solution.py:24
  201.4 36.0 %collective-permute-start.35 = (bf16[1024,512]{1,0:T(8,128)(2,1)}, bf16[1024,512]{1,0:T(8,128)(2,1)}, u32[]{:S(2)}, u32[]{:S(2)}) collective-permute-start(bf16[1024,512]{1,0:T(8,128)(2,1)} %get-tuple-element.140), channel_id=1, source_target_pairs={{0,4},{2,6},{4,0},{6,2},{1,5},{3,7},{5,1},{7,3},{8,12},{10,14},{12... | collective-permute-start | bytes 3145736 | tf_op jit(solution)/shard_map/ppermute | solution.py:24
  211.9 21.3 %collective-permute-start.43 = (bf16[1024,128]{1,0:T(8,128)(2,1)S(1)}, bf16[1024,128]{1,0:T(8,128)(2,1)S(1)}, u32[]{:S(2)}, u32[]{:S(2)}) collective-permute-start(bf16[1024,128]{1,0:T(8,128)(2,1)S(1)} %add_convert_fusion), channel_id=1, source_target_pairs={{0,16},{8,24},{16,0},{24,8},{1,17},{9,25},{17,1},{25,9},{2,18},{10... | collective-permute-start | bytes 786440 | tf_op jit(solution)/shard_map/ppermute | solution.py:24
  211.9 21.3 %collective-permute-start.42 = (bf16[1024,128]{1,0:T(8,128)(2,1)S(1)}, bf16[1024,128]{1,0:T(8,128)(2,1)S(1)}, u32[]{:S(2)}, u32[]{:S(2)}) collective-permute-start(bf16[1024,128]{1,0:T(8,128)(2,1)S(1)} %add_convert_fusion), channel_id=1, source_target_pairs={{0,8},{8,0},{16,24},{24,16},{1,9},{9,1},{17,25},{25,17},{2,10},{10... | collective-permute-start | bytes 786440 | tf_op jit(solution)/shard_map/ppermute | solution.py:24
  214.7 22.7 %all-to-all-start.1 = ((bf16[4,1024,128]{2,1,0:T(8,128)(2,1)}), bf16[4,1024,128]{2,1,0:T(8,128)(2,1)}, u32[]{:S(2)}, u32[]{:S(2)}) async-start(bf16[4,1024,128]{2,1,0:T(8,128)(2,1)} %broadcast_in_dim.95), calls=%async_computation.1 | async-start | bytes 2097152 | tf_op jit(solution)/shard_map/all_to_all | solution.py:28
  238.0 20.0 %collective-permute-start.48 = (bf16[3072,128]{1,0:T(8,128)(2,1)S(1)}, bf16[3072,128]{1,0:T(8,128)(2,1)}, u32[]{:S(2)}, u32[]{:S(2)}) collective-permute-start(bf16[3072,128]{1,0:T(8,128)(2,1)S(1)} %pad_maximum_fusion.4.refs_0_), channel_id=1, source_target_pairs={{0,2},{2,0},{4,6},{6,4},{1,3},{3,1},{5,7},{7,5},{8,10},{10,8},{12,... | collective-permute-start | bytes 2359304 | tf_op jit(solution)/shard_map/ppermute | solution.py:24
  239.6 29.0 %collective-permute-start.50 = (bf16[4,1024,128]{2,1,0:T(8,128)(2,1)}, bf16[4,1024,128]{2,1,0:T(8,128)(2,1)}, u32[]{:S(2)}, u32[]{:S(2)}) collective-permute-start(bf16[4,1024,128]{2,1,0:T(8,128)(2,1)} %all-to-all-done.1.near_ref), channel_id=1, source_target_pairs={{0,1},{1,0},{2,3},{3,2},{4,5},{5,4},{6,7},{7,6},{8,9},{9,8},{10,11... | collective-permute-start | bytes 3145736 | tf_op jit(solution)/shard_map/ppermute | solution.py:24
  258.0 25.3 %collective-permute-start.51 = (bf16[3072,128]{1,0:T(8,128)(2,1)S(1)}, bf16[3072,128]{1,0:T(8,128)(2,1)S(1)}, u32[]{:S(2)}, u32[]{:S(2)}) collective-permute-start(bf16[3072,128]{1,0:T(8,128)(2,1)S(1)} %pad_maximum_fusion.4.refs_0_), channel_id=1, source_target_pairs={{0,1},{1,0},{2,3},{3,2},{4,5},{5,4},{6,7},{7,6},{8,9},{9,8},{10,11... | collective-permute-start | bytes 2359304 | tf_op jit(solution)/shard_map/ppermute | solution.py:24
  263.0 20.3 %collective-permute-start.53 = (bf16[3072,128]{1,0:T(8,128)(2,1)}, bf16[3072,128]{1,0:T(8,128)(2,1)S(1)}, u32[]{:S(2)}, u32[]{:S(2)}) collective-permute-start(bf16[3072,128]{1,0:T(8,128)(2,1)} %collective-permute-done.49.refs_2_), channel_id=1, source_target_pairs={{0,1},{1,0},{2,3},{3,2},{4,5},{5,4},{6,7},{7,6},{8,9},{9,8},{10,11... | collective-permute-start | bytes 2359304 | tf_op jit(solution)/shard_map/ppermute | solution.py:24
  (95 other events, 888.7 us)

commit v3 on v2

--- a/solution.py
+++ b/solution.py
@@ -509,17 +509,18 @@
                 seen = k_iota + j * rows >= starts_ref[:, here]
                 if i == j:
                     seen = seen & (k_iota <= q_iota)
-                dq = None
+                lows = []
+                slopes = []
                 for h in range(2):
                     weights = jnp.where(seen, jnp.exp(matmul_nt(k2, qs[h])), 0.0)
                     slope = matmul_nt(v2, dos[h]) - sh_ref[h : h + 1, here]
-                    ds = (weights * slope).astype(BF16)
-                    dv_part = matmul(weights.astype(BF16), dos[h])
-                    dk_part = matmul(ds, qs[h])
-                    dq_part = matmul_tn(ds, ks[h])
-                    dv = dv_part if dv is None else dv + dv_part
-                    dk = dk_part if dk is None else dk + dk_part
-                    dq = dq_part if dq is None else dq + dq_part
+                    slopes.append((weights * slope).astype(BF16))
+                    lows.append(weights.astype(BF16))
+                dv_part = matmul(jnp.concatenate(lows, axis=1), jnp.concatenate(dos, axis=0))
+                dk_part = matmul(jnp.concatenate(slopes, axis=1), jnp.concatenate(qs, axis=0))
+                dq = matmul_tn(jnp.concatenate(slopes, axis=0), jnp.concatenate(ks, axis=0))
+                dv = dv_part if dv is None else dv + dv_part
+                dk = dk_part if dk is None else dk + dk_part
                 if j == 0:
                     dq_ref[here, :] = dq
                 else:

time: 291 us -> 289 us (level)
  no operation moved by 1% of the time
where the time goes in v3:
time: 289 us
  waiting for transfers between devices  98.4 us (34%)
  Pallas kernels  74.2 us (26%)
  starting transfers between devices  70 us (24%)
  local copies, waits for them, and re-layouts  21.7 us (8%)
  other arithmetic  19.9 us (7%)
  matrix products  2.94 us (1%)
    ppermute x58, waiting for transfers between devices, swap(): return lax.ppermute(value, axis, [(i, i ^ bits) for i in range(size)])  86.2 us
    ppermute x58, starting transfers between devices, swap(): return lax.ppermute(value, axis, [(i, i ^ bits) for i in range(size)])  62 us
    pallas_call x1, Pallas kernels, attend_backward(): pl.pallas_call(functools.partial(backward_kernel, n=n, rows=rows, owners=...  15.1 us
    pallas_call x2, Pallas kernels, dense_out(): pl.pallas_call(functools.partial(dense_out_kernel, counts=counts, s=s, n=...  12.8 us
    all_to_all x2, waiting for transfers between devices, exchange(): return lax.all_to_all(value, axis, split_axis=0, concat_axis=0, tiled=True)  12.2 us
    pallas_call x1, Pallas kernels, attend_forward(): pl.pallas_call(functools.partial(forward_kernel, n=n, rows=rows), out_sha...  10.6 us
    pallas_call x2, Pallas kernels, expert_rows(): pl.pallas_call(functools.partial(expert_kernel, m=m), out_shape=[shaped((...  10.4 us
    all_to_all x2, starting transfers between devices, exchange(): return lax.all_to_all(value, axis, split_axis=0, concat_axis=0, tiled=True)  8.07 us
  transfers between devices with their start and end apart: 60, of which 27 were waited for; matrix products, arithmetic and copies ran while one was open for 12% of the time, Pallas kernels for 24%

profile of v3, /device:TPU:0, one launch (start us, length us, event | category | flops | bytes accessed | tf_op | source)
XLA Modules:
  0.0 288.7 jit_solution(15710379878718091306)
XLA Ops:
  10.7 4.0 %collective-permute-start.17 = (bf16[80,1024]{1,0:T(8,128)(2,1)}, bf16[80,1024]{1,0:T(8,128)(2,1)}, u32[]{:S(2)}, u32[]{:S(2)}) collective-permute-start(bf16[80,1024]{1,0:T(8,128)(2,1)} %get-tuple-element.188), channel_id=1, source_target_pairs={{0,24},{8,16},{16,8},{24,0},{1,25},{9,17},{17,9},{25,1},{2,26},{10... | collective-permute-start | bytes 491528 | tf_op jit(solution)/shard_map/ppermute | solution.py:24
  18.9 9.5 %collective-permute-done.2.refs_3_ = bf16[256,1024]{1,0:T(8,128)(2,1)S(1)} collective-permute-done((bf16[256,1024]{1,0:T(8,128)(2,1)S(1)}, bf16[256,1024]{1,0:T(8,128)(2,1)S(1)}, u32[]{:S(2)}, u32[]{:S(2)}) %collective-permute-start.2) | collective-permute-done | bytes 524320 | tf_op jit(solution)/shard_map/ppermute | solution.py:24
  34.3 10.6 %shard_map.170 = (bf16[1024,1024]{1,0:T(8,128)(2,1)}, f32[256,1]{1,0:T(8,128)S(1)}, bf16[1024,256]{1,0:T(8,128)(2,1)S(1)}, bf16[1024,256]{1,0:T(8,128)(2,1)S(1)}...) custom-call(s32[3]{0:T(128)S(1)} %pad_add_fusion.ids_ref, ...), custom_call_target="tpu_custom_call" | custom-call | flops 738197504 | bytes 2490368 | tf_op jit(solution)/shard_map/pallas_call | solution.py:140
  64.4 4.4 %collective-permute-done.18 = bf16[320,1024]{1,0:T(8,128)(2,1)S(1)} collective-permute-done((bf16[320,1024]{1,0:T(8,128)(2,1)S(1)}, bf16[320,1024]{1,0:T(8,128)(2,1)S(1)}, u32[]{:S(2)}, u32[]{:S(2)}) %collective-permute-start.18) | collective-permute-done | bytes 655392 | tf_op jit(solution)/shard_map/ppermute | solution.py:24
  71.6 4.1 %collective-permute-done.7 = bf16[80,1024]{1,0:T(8,128)(2,1)S(1)} collective-permute-done((bf16[80,1024]{1,0:T(8,128)(2,1)S(1)}, bf16[80,1024]{1,0:T(8,128)(2,1)S(1)}, u32[]{:S(2)}, u32[]{:S(2)}) %collective-permute-start.7) | collective-permute-done | bytes 163872 | tf_op jit(solution)/shard_map/ppermute | solution.py:24
  77.8 8.6 %collective-permute-done.12 = bf16[160,1024]{1,0:T(8,128)(2,1)S(1)} collective-permute-done((bf16[160,1024]{1,0:T(8,128)(2,1)S(1)}, bf16[160,1024]{1,0:T(8,128)(2,1)S(1)}, u32[]{:S(2)}, u32[]{:S(2)}) %collective-permute-start.12) | collective-permute-done | bytes 327712 | tf_op jit(solution)/shard_map/ppermute | solution.py:24
  86.6 5.5 %collective-permute-done.8 = bf16[160,1024]{1,0:T(8,128)(2,1)S(1)} collective-permute-done((bf16[160,1024]{1,0:T(8,128)(2,1)S(1)}, bf16[160,1024]{1,0:T(8,128)(2,1)S(1)}, u32[]{:S(2)}, u32[]{:S(2)}) %collective-permute-start.8) | collective-permute-done | bytes 327712 | tf_op jit(solution)/shard_map/ppermute | solution.py:24
  92.6 5.1 %shard_map.172 = (bf16[320,1024]{1,0:T(8,128)(2,1)S(1)}, bf16[320,1024]{1,0:T(8,128)(2,1)S(1)}, bf16[640,1024]{1,0:T(8,128)(2,1)S(1)}, bf16[640,1024]{1,0:T(8,128)(2,1)S(1)}) custom-call(bf16[640,1024]{1,0:T(8,128)(2,1)S(1)} %constant_dynamic-update-slice_fusion.refs_0_.refs_1_, bf16[640,1024]{1,0:T(8,128)(2,1)S(1)} %bitcast.66, ...), custom_call_target="tpu_custom_call" | custom-call | flops 1006632960 | bytes 2359296 | tf_op jit(solution)/shard_map/pallas_call | solution.py:254
  98.4 5.3 %shard_map.173 = (bf16[320,1024]{1,0:T(8,128)(2,1)S(1)}, bf16[320,1024]{1,0:T(8,128)(2,1)S(1)}, bf16[640,1024]{1,0:T(8,128)(2,1)S(1)}, bf16[640,1024]{1,0:T(8,128)(2,1)S(1)}) custom-call(bf16[640,1024]{1,0:T(8,128)(2,1)S(1)} %pad_maximum_fusion.1.refs_0_, bf16[640,1024]{1,0:T(8,128)(2,1)S(1)} %bitcast.64, bf16[1024,512]{1,0:T(8,128)(2,1)S(1)} %bitcast.69, ...), custom_call_target="tpu_custom_call" | custom-call | flops 1006632960 | bytes 2359296 | tf_op jit(solution)/shard_map/pallas_call | solution.py:254
  107.7 4.6 %shard_map.177 = (f32[512,1024]{1,0:T(8,128)S(1)}, bf16[512,1024]{1,0:T(8,128)(2,1)S(1)}) custom-call(bf16[640,1024]{1,0:T(8,128)(2,1)S(1)} %get-tuple-element.127.refs_0_, bf16[640,1024]{1,0:T(8,128)(2,1)S(1)} %get-tuple-element.128.refs_1_, bf16[640,1024]{1,0:T(8,128)(2,1)S(1)} %bitcast.65, bf16[640,1024]{1,0:T(8,128)(2,1)S(1)} %bitcast.67), custom_call_target="tpu_custom_call" | custom-call | flops 671088640 | bytes 2097152 | tf_op jit(solution)/shard_map/pallas_call | solution.py:400
  122.9 5.1 %shard_map.174 = (f32[1024,512]{1,0:T(8,128)S(1)}, bf16[1024,512]{1,0:T(8,128)(2,1)}) custom-call(bf16[640,1024]{1,0:T(8,128)(2,1)S(1)} %pad_maximum_fusion.1.refs_0_, bf16[640,1024]{1,0:T(8,128)(2,1)S(1)} %constant_dynamic-update-slice_fusion.refs_0_.refs_1_, bf16[640,1024]{1,0:T(8,128)(2,1)S(1)} %get-tuple-element.105.refs_2_, ...), custom_call_target="tpu_custom_call" | custom-call | flops 671088640 | bytes 2097152 | tf_op jit(solution)/shard_map/pallas_call | solution.py:355
  129.4 4.9 %shard_map.175 = (bf16[2,320,1024]{2,1,0:T(8,128)(2,1)S(1)}, bf16[2,320,1024]{2,1,0:T(8,128)(2,1)}) custom-call(bf16[640,1024]{1,0:T(8,128)(2,1)S(1)} %get-tuple-element.127.refs_0_, bf16[640,1024]{1,0:T(8,128)(2,1)S(1)} %get-tuple-element.128.refs_1_, bf16[512,1024]{1,0:T(8,128)(2,1)S(1)} %bitcast.63, ...), custom_call_target="tpu_custom_call" | custom-call | flops 671088640 | bytes 1835008 | tf_op jit(solution)/shard_map/pallas_call | solution.py:448
  135.3 4.2 %shard_map.176 = (f32[256,1024]{1,0:T(8,128)S(1)}, bf16[4,256,256]{2,1,0:T(8,128)(2,1)S(1)}, f32[4096,128]{1,0:T(8,128)S(1)}, bf16[4112,128]{1,0:T(8,128)(2,1)S(1)}) custom-call(s32[3]{0:T(128)S(1)} %pad_add_fusion.ids_ref, bf16[80,1024]{1,0:T(8,128)(2,1)S(1)} %get-tuple-element.121.refs_0_, bf16[80,1024]{1,0:T(8,128)(2,1)S(1)} %collective-permute-done.22.refs_1_, ...), custom_call_target="tpu_custom_call" | custom-call | flops 335544320 | bytes 2621440 | tf_op jit(solution)/shard_map/pallas_call | solution.py:321
  143.2 3.8 %collective-permute-done.30 = bf16[256,256]{1,0:T(8,128)(2,1)S(1)} collective-permute-done((bf16[256,256]{1,0:T(8,128)(2,1)S(1)}, bf16[256,256]{1,0:T(8,128)(2,1)S(1)}, u32[]{:S(2)}, u32[]{:S(2)}) %collective-permute-start.30) | collective-permute-done | bytes 131104 | tf_op jit(solution)/shard_map/ppermute | solution.py:24
  154.8 15.1 %shard_map.178 = (bf16[4,3,256,256]{3,2,1,0:T(8,128)(2,1)}, f32[4,768,128]{2,1,0:T(8,128)}, bf16[4,768,128]{2,1,0:T(8,128)(2,1)S(1)}) custom-call(s32[3]{0:T(128)S(1)} %pad_add_fusion.ids_ref, s32[1,1024]{1,0:T(1,128)S(1)} %bitcast.81, bf16[1024,1024]{1,0:T(8,128)(2,1)} %get-tuple-element.109.normed_ref, bf16[1024,256]{1,0:T(8,128)(2,1)S(1)} %copy-done.24, ...), custom_call_target="tpu_custom_call" | custom-call | flops 1241513984 | bytes 2686976 | tf_op jit(solution)/shard_map/pallas_call | solution.py:559
  170.7 3.6 %all-to-all-start = ((bf16[4,3,256,256]{3,2,1,0:T(8,128)(2,1)}), bf16[4,3,256,256]{3,2,1,0:T(8,128)(2,1)S(1)}, u32[]{:S(2)}, u32[]{:S(2)}) async-start(bf16[4,3,256,256]{3,2,1,0:T(8,128)(2,1)} %get-tuple-element.139), calls=%async_computation | async-start | bytes 3145728 | tf_op jit(solution)/shard_map/all_to_all | solution.py:28
  183.8 10.6 %all-to-all-done.d_ref = bf16[4,3,256,256]{3,2,1,0:T(8,128)(2,1)S(1)} async-done(((bf16[4,3,256,256]{3,2,1,0:T(8,128)(2,1)}), bf16[4,3,256,256]{3,2,1,0:T(8,128)(2,1)S(1)}, u32[]{:S(2)}, u32[]{:S(2)}) %all-to-all-start) | async-done | bytes 1572896 | tf_op jit(solution)/shard_map/all_to_all | solution.py:28
  200.3 6.0 %collective-permute-done.40 = bf16[1040,128]{1,0:T(8,128)(2,1)S(1)} collective-permute-done((bf16[1040,128]{1,0:T(8,128)(2,1)}, bf16[1040,128]{1,0:T(8,128)(2,1)S(1)}, u32[]{:S(2)}, u32[]{:S(2)}) %collective-permute-start.40) | collective-permute-done | bytes 266272 | tf_op jit(solution)/shard_map/ppermute | solution.py:24
  213.0 4.5 %all-to-all-start.1 = ((bf16[4,1024,128]{2,1,0:T(8,128)(2,1)}), bf16[4,1024,128]{2,1,0:T(8,128)(2,1)}, u32[]{:S(2)}, u32[]{:S(2)}) async-start(bf16[4,1024,128]{2,1,0:T(8,128)(2,1)} %broadcast_in_dim.95), calls=%async_computation.1 | async-start | bytes 2097152 | tf_op jit(solution)/shard_map/all_to_all | solution.py:28
  218.6 12.9 %collective-permute-done.43 = bf16[1024,128]{1,0:T(8,128)(2,1)S(1)} collective-permute-done((bf16[1024,128]{1,0:T(8,128)(2,1)S(1)}, bf16[1024,128]{1,0:T(8,128)(2,1)S(1)}, u32[]{:S(2)}, u32[]{:S(2)}) %collective-permute-start.43) | collective-permute-done | bytes 262176 | tf_op jit(solution)/shard_map/ppermute | solution.py:24
  242.5 11.4 %collective-permute-done.49.refs_2_ = bf16[3072,128]{1,0:T(8,128)(2,1)} collective-permute-done((bf16[3072,128]{1,0:T(8,128)(2,1)S(1)}, bf16[3072,128]{1,0:T(8,128)(2,1)}, u32[]{:S(2)}, u32[]{:S(2)}) %collective-permute-start.49) | collective-permute-done | bytes 786464 | tf_op jit(solution)/shard_map/ppermute | solution.py:24
  267.5 4.0 %shard_map.180 = f32[256,1024]{1,0:T(8,128)} custom-call(bf16[4,3,256,256]{3,2,1,0:T(8,128)(2,1)S(1)} %copy-done.6, bf16[1024,3072]{1,0:T(8,128)(2,1)S(1)} %bitcast.57, bf16[256,1024]{1,0:T(8,128)(2,1)S(1)} %bitcast.75, f32[256,1]{1,0:T(8,128)S(1)} %copy-done.36, f32[1,1024]{1,0:T(1,128)S(1)} %bitcast.78, f32[256,1024]{1,0:T(8,128)S(1)} %copy-done.17), custom_call_target="tpu_custom_call" | custom-call | flops 402653184 | bytes 2621440 | tf_op jit(solution)/shard_map/pallas_call | solution.py:765
  275.0 6.6 %shard_map.181 = (f32[1024,3072]{1,0:T(8,128)}, f32[1024,1024]{1,0:T(8,128)}, f32[1024,128]{1,0:T(8,128)S(1)}) custom-call(s32[3]{0:T(128)S(1)} %pad_add_fusion.ids_ref, bf16[4,1024,128]{2,1,0:T(8,128)(2,1)} %all-to-all-done.1.near_ref, bf16[3072,128]{1,0:T(8,128)(2,1)S(1)} %pad_maximum_fusion.4.refs_0_, bf16[3072,128]{1,0:T(8,128)(2,1)} %collective-permute-done.48.refs_1_, ...), custom_call_target="tpu_custom_call" | custom-call | flops 786432 | bytes 4194304 | tf_op jit(solution)/shard_map/pallas_call | solution.py:708
  281.7 6.2 %shard_map.182 = (f32[1024,3072]{1,0:T(8,128)}, f32[1024,1024]{1,0:T(8,128)}, f32[1024,128]{1,0:T(8,128)S(1)}) custom-call(s32[3]{0:T(128)S(1)} %pad_add_fusion.ids_ref, bf16[4,1024,128]{2,1,0:T(8,128)(2,1)} %collective-permute-done.50.near_ref, ...), custom_call_target="tpu_custom_call", output_to_operand_aliasing={{0}: (8, {}), {1}: (9, {}), {2}: (10, {})} | custom-call | flops 786432 | bytes 4194304 | tf_op jit(solution)/shard_map/pallas_call | solution.py:708
  (294 shorter events, 126.8 us)
Async XLA Ops:
  9.7 18.7 %collective-permute-start.2 = (bf16[256,1024]{1,0:T(8,128)(2,1)S(1)}, bf16[256,1024]{1,0:T(8,128)(2,1)S(1)}, u32[]{:S(2)}, u32[]{:S(2)}) collective-permute-start(bf16[256,1024]{1,0:T(8,128)(2,1)S(1)} %bitcast.72), channel_id=1, source_target_pairs={{0,6},{2,4},{4,2},{6,0},{1,7},{3,5},{5,3},{7,1},{8,14},{10,12},{12... | collective-permute-start | bytes 1572872 | tf_op jit(solution)/shard_map/ppermute | solution.py:24
  10.7 22.2 %collective-permute-start.17 = (bf16[80,1024]{1,0:T(8,128)(2,1)}, bf16[80,1024]{1,0:T(8,128)(2,1)}, u32[]{:S(2)}, u32[]{:S(2)}) collective-permute-start(bf16[80,1024]{1,0:T(8,128)(2,1)} %get-tuple-element.188), channel_id=1, source_target_pairs={{0,24},{8,16},{16,8},{24,0},{1,25},{9,17},{17,9},{25,1},{2,26},{10... | collective-permute-start | bytes 491528 | tf_op jit(solution)/shard_map/ppermute | solution.py:24
  14.7 18.3 %collective-permute-start.16 = (bf16[80,1024]{1,0:T(8,128)(2,1)}, bf16[80,1024]{1,0:T(8,128)(2,1)}, u32[]{:S(2)}, u32[]{:S(2)}) collective-permute-start(bf16[80,1024]{1,0:T(8,128)(2,1)} %get-tuple-element.189), channel_id=1, source_target_pairs={{0,16},{8,24},{16,0},{24,8},{1,17},{9,25},{17,1},{25,9},{2,18},{10... | collective-permute-start | bytes 491528 | tf_op jit(solution)/shard_map/ppermute | solution.py:24
  29.1 18.7 %collective-permute-start.3 = (bf16[768,512]{1,0:T(8,128)(2,1)}, bf16[768,512]{1,0:T(8,128)(2,1)S(1)}, u32[]{:S(2)}, u32[]{:S(2)}) collective-permute-start(bf16[768,512]{1,0:T(8,128)(2,1)} %slice_bitcast_fusion.1), channel_id=1, source_target_pairs={{0,4},{2,6},{4,0},{6,2},{1,5},{3,7},{5,1},{7,3},{8,12},{10,14},{12... | collective-permute-start | bytes 2359304 | tf_op jit(solution)/shard_map/ppermute | solution.py:24
  58.0 28.5 %collective-permute-start.13 = (bf16[1280,512]{1,0:T(8,128)(2,1)S(1)}, bf16[1280,512]{1,0:T(8,128)(2,1)S(1)}, u32[]{:S(2)}, u32[]{:S(2)}) collective-permute-start(bf16[1280,512]{1,0:T(8,128)(2,1)S(1)} %pad_maximum_fusion.2), channel_id=1, source_target_pairs={{0,4},{2,6},{4,0},{6,2},{1,5},{3,7},{5,1},{7,3},{8,12},{10,14},{12... | collective-permute-start | bytes 3932168 | tf_op jit(solution)/shard_map/ppermute | solution.py:24
  69.0 23.3 %collective-permute-start.19 = (bf16[2,320,1024]{2,1,0:T(8,128)(2,1)S(1)}, bf16[2,320,1024]{2,1,0:T(8,128)(2,1)S(1)}, u32[]{:S(2)}, u32[]{:S(2)}) collective-permute-start(bf16[2,320,1024]{2,1,0:T(8,128)(2,1)S(1)} %get-tuple-element.176), channel_id=1, source_target_pairs={{0,1},{1,0},{2,3},{3,2},{4,5},{5,4},{6,7},{7,6},{8,9},{9,8},{10,11... | collective-permute-start | bytes 3932168 | tf_op jit(solution)/shard_map/ppermute | solution.py:24
  112.2 27.3 %collective-permute-start.27 = (bf16[512,1024]{1,0:T(8,128)(2,1)S(1)}, bf16[512,1024]{1,0:T(8,128)(2,1)S(1)}, u32[]{:S(2)}, u32[]{:S(2)}) collective-permute-start(bf16[512,1024]{1,0:T(8,128)(2,1)S(1)} %get-tuple-element.129), channel_id=1, source_target_pairs={{0,4},{2,6},{4,0},{6,2},{1,5},{3,7},{5,1},{7,3},{8,12},{10,14},{12... | collective-permute-start | bytes 3145736 | tf_op jit(solution)/shard_map/ppermute | solution.py:24
  114.7 19.5 %collective-permute-start.26 = (bf16[80,1024]{1,0:T(8,128)(2,1)S(1)}, bf16[80,1024]{1,0:T(8,128)(2,1)S(1)}, u32[]{:S(2)}, u32[]{:S(2)}) collective-permute-start(bf16[80,1024]{1,0:T(8,128)(2,1)S(1)} %get-tuple-element.203), channel_id=1, source_target_pairs={{0,24},{8,16},{16,8},{24,0},{1,25},{9,17},{17,9},{25,1},{2,26},{10... | collective-permute-start | bytes 491528 | tf_op jit(solution)/shard_map/ppermute | solution.py:24
  151.2 18.7 %collective-permute-start.32 = (bf16[1040,128]{1,0:T(8,128)(2,1)S(1)}, bf16[1040,128]{1,0:T(8,128)(2,1)S(1)}, u32[]{:S(2)}, u32[]{:S(2)}) collective-permute-start(bf16[1040,128]{1,0:T(8,128)(2,1)S(1)} %get-tuple-element.133), channel_id=1, source_target_pairs={{0,2},{2,0},{4,6},{6,4},{1,3},{3,1},{5,7},{7,5},{8,10},{10,8},{12,... | collective-permute-start | bytes 798728 | tf_op jit(solution)/shard_map/ppermute | solution.py:24
  154.7 29.1 %collective-permute-start.36 = (bf16[2,320,1024]{2,1,0:T(8,128)(2,1)}, bf16[2,320,1024]{2,1,0:T(8,128)(2,1)}, u32[]{:S(2)}, u32[]{:S(2)}) collective-permute-start(bf16[2,320,1024]{2,1,0:T(8,128)(2,1)} %get-tuple-element.141), channel_id=1, source_target_pairs={{0,1},{1,0},{2,3},{3,2},{4,5},{5,4},{6,7},{7,6},{8,9},{9,8},{10,11... | collective-permute-start | bytes 3932168 | tf_op jit(solution)/shard_map/ppermute | solution.py:24
  170.7 23.7 %all-to-all-start = ((bf16[4,3,256,256]{3,2,1,0:T(8,128)(2,1)}), bf16[4,3,256,256]{3,2,1,0:T(8,128)(2,1)S(1)}, u32[]{:S(2)}, u32[]{:S(2)}) async-start(bf16[4,3,256,256]{3,2,1,0:T(8,128)(2,1)} %get-tuple-element.139), calls=%async_computation | async-start | bytes 3145728 | tf_op jit(solution)/shard_map/all_to_all | solution.py:28
  179.4 20.9 %collective-permute-start.39 = (bf16[1040,128]{1,0:T(8,128)(2,1)}, bf16[1040,128]{1,0:T(8,128)(2,1)S(1)}, u32[]{:S(2)}, u32[]{:S(2)}) collective-permute-start(bf16[1040,128]{1,0:T(8,128)(2,1)} %get-tuple-element.146), channel_id=1, source_target_pairs={{0,24},{8,16},{16,8},{24,0},{1,25},{9,17},{17,9},{25,1},{2,26},{10... | collective-permute-start | bytes 798728 | tf_op jit(solution)/shard_map/ppermute | solution.py:24
  181.9 24.4 %collective-permute-start.40 = (bf16[1040,128]{1,0:T(8,128)(2,1)}, bf16[1040,128]{1,0:T(8,128)(2,1)S(1)}, u32[]{:S(2)}, u32[]{:S(2)}) collective-permute-start(bf16[1040,128]{1,0:T(8,128)(2,1)} %get-tuple-element.147), channel_id=1, source_target_pairs={{0,16},{8,24},{16,0},{24,8},{1,17},{9,25},{17,1},{25,9},{2,18},{10... | collective-permute-start | bytes 798728 | tf_op jit(solution)/shard_map/ppermute | solution.py:24
  182.0 24.2 %collective-permute-start.41 = (bf16[1040,128]{1,0:T(8,128)(2,1)}, bf16[1040,128]{1,0:T(8,128)(2,1)}, u32[]{:S(2)}, u32[]{:S(2)}) collective-permute-start(bf16[1040,128]{1,0:T(8,128)(2,1)} %get-tuple-element.148), channel_id=1, source_target_pairs={{0,8},{8,0},{16,24},{24,16},{1,9},{9,1},{17,25},{25,17},{2,10},{10... | collective-permute-start | bytes 798728 | tf_op jit(solution)/shard_map/ppermute | solution.py:24
  198.3 33.3 %collective-permute-start.37 = (bf16[320,1024]{1,0:T(8,128)(2,1)}, bf16[320,1024]{1,0:T(8,128)(2,1)}, u32[]{:S(2)}, u32[]{:S(2)}) collective-permute-start(bf16[320,1024]{1,0:T(8,128)(2,1)} %fusion.4), channel_id=1, source_target_pairs={{0,2},{2,0},{4,6},{6,4},{1,3},{3,1},{5,7},{7,5},{8,10},{10,8},{12,... | collective-permute-start | bytes 1966088 | tf_op jit(solution)/shard_map/ppermute | solution.py:24
  199.7 36.0 %collective-permute-start.35 = (bf16[1024,512]{1,0:T(8,128)(2,1)}, bf16[1024,512]{1,0:T(8,128)(2,1)}, u32[]{:S(2)}, u32[]{:S(2)}) collective-permute-start(bf16[1024,512]{1,0:T(8,128)(2,1)} %get-tuple-element.140), channel_id=1, source_target_pairs={{0,4},{2,6},{4,0},{6,2},{1,5},{3,7},{5,1},{7,3},{8,12},{10,14},{12... | collective-permute-start | bytes 3145736 | tf_op jit(solution)/shard_map/ppermute | solution.py:24
  210.2 21.3 %collective-permute-start.43 = (bf16[1024,128]{1,0:T(8,128)(2,1)S(1)}, bf16[1024,128]{1,0:T(8,128)(2,1)S(1)}, u32[]{:S(2)}, u32[]{:S(2)}) collective-permute-start(bf16[1024,128]{1,0:T(8,128)(2,1)S(1)} %add_convert_fusion), channel_id=1, source_target_pairs={{0,16},{8,24},{16,0},{24,8},{1,17},{9,25},{17,1},{25,9},{2,18},{10... | collective-permute-start | bytes 786440 | tf_op jit(solution)/shard_map/ppermute | solution.py:24
  210.2 21.3 %collective-permute-start.42 = (bf16[1024,128]{1,0:T(8,128)(2,1)S(1)}, bf16[1024,128]{1,0:T(8,128)(2,1)S(1)}, u32[]{:S(2)}, u32[]{:S(2)}) collective-permute-start(bf16[1024,128]{1,0:T(8,128)(2,1)S(1)} %add_convert_fusion), channel_id=1, source_target_pairs={{0,8},{8,0},{16,24},{24,16},{1,9},{9,1},{17,25},{25,17},{2,10},{10... | collective-permute-start | bytes 786440 | tf_op jit(solution)/shard_map/ppermute | solution.py:24
  213.0 22.8 %all-to-all-start.1 = ((bf16[4,1024,128]{2,1,0:T(8,128)(2,1)}), bf16[4,1024,128]{2,1,0:T(8,128)(2,1)}, u32[]{:S(2)}, u32[]{:S(2)}) async-start(bf16[4,1024,128]{2,1,0:T(8,128)(2,1)} %broadcast_in_dim.95), calls=%async_computation.1 | async-start | bytes 2097152 | tf_op jit(solution)/shard_map/all_to_all | solution.py:28
  235.8 18.1 %collective-permute-start.49 = (bf16[3072,128]{1,0:T(8,128)(2,1)S(1)}, bf16[3072,128]{1,0:T(8,128)(2,1)}, u32[]{:S(2)}, u32[]{:S(2)}) collective-permute-start(bf16[3072,128]{1,0:T(8,128)(2,1)S(1)} %pad_maximum_fusion.4.refs_0_), channel_id=1, source_target_pairs={{0,4},{2,6},{4,0},{6,2},{1,5},{3,7},{5,1},{7,3},{8,12},{10,14},{12... | collective-permute-start | bytes 2359304 | tf_op jit(solution)/shard_map/ppermute | solution.py:24
  236.3 20.0 %collective-permute-start.48 = (bf16[3072,128]{1,0:T(8,128)(2,1)S(1)}, bf16[3072,128]{1,0:T(8,128)(2,1)}, u32[]{:S(2)}, u32[]{:S(2)}) collective-permute-start(bf16[3072,128]{1,0:T(8,128)(2,1)S(1)} %pad_maximum_fusion.4.refs_0_), channel_id=1, source_target_pairs={{0,2},{2,0},{4,6},{6,4},{1,3},{3,1},{5,7},{7,5},{8,10},{10,8},{12,... | collective-permute-start | bytes 2359304 | tf_op jit(solution)/shard_map/ppermute | solution.py:24
  238.0 29.0 %collective-permute-start.50 = (bf16[4,1024,128]{2,1,0:T(8,128)(2,1)}, bf16[4,1024,128]{2,1,0:T(8,128)(2,1)}, u32[]{:S(2)}, u32[]{:S(2)}) collective-permute-start(bf16[4,1024,128]{2,1,0:T(8,128)(2,1)} %all-to-all-done.1.near_ref), channel_id=1, source_target_pairs={{0,1},{1,0},{2,3},{3,2},{4,5},{5,4},{6,7},{7,6},{8,9},{9,8},{10,11... | collective-permute-start | bytes 3145736 | tf_op jit(solution)/shard_map/ppermute | solution.py:24
  256.3 25.3 %collective-permute-start.51 = (bf16[3072,128]{1,0:T(8,128)(2,1)S(1)}, bf16[3072,128]{1,0:T(8,128)(2,1)S(1)}, u32[]{:S(2)}, u32[]{:S(2)}) collective-permute-start(bf16[3072,128]{1,0:T(8,128)(2,1)S(1)} %pad_maximum_fusion.4.refs_0_), channel_id=1, source_target_pairs={{0,1},{1,0},{2,3},{3,2},{4,5},{5,4},{6,7},{7,6},{8,9},{9,8},{10,11... | collective-permute-start | bytes 2359304 | tf_op jit(solution)/shard_map/ppermute | solution.py:24
  261.4 20.3 %collective-permute-start.53 = (bf16[3072,128]{1,0:T(8,128)(2,1)}, bf16[3072,128]{1,0:T(8,128)(2,1)S(1)}, u32[]{:S(2)}, u32[]{:S(2)}) collective-permute-start(bf16[3072,128]{1,0:T(8,128)(2,1)} %collective-permute-done.49.refs_2_), channel_id=1, source_target_pairs={{0,1},{1,0},{2,3},{3,2},{4,5},{5,4},{6,7},{7,6},{8,9},{9,8},{10,11... | collective-permute-start | bytes 2359304 | tf_op jit(solution)/shard_map/ppermute | solution.py:24
  (95 other events, 886.2 us)
